TPU v7x, 256 devices: a whole 4x4x8 slice. The times are simulated.
256 devices in a mesh: src: 16 (over y, x_hi, core), tgt: 16 (over z, x_lo).
Axes of the slice: x: 4 (x_hi: 2, x_lo: 2; x = x_hi * 2 + x_lo), y: 4, z: 8, core: 2. Of those that a mesh axis runs over, the one named last changes fastest.
Arguments:
- edge_feat: bfloat16 [16, 16, 2048, 512], P('src', 'tgt'), may hold values from -6 to 6
- tile_counts: int32 [16, 16], P('src', 'tgt'), may hold values from 512 to 2048, as said below
- reverse_rows: int32 [16, 16, 2048], P('src', 'tgt'), may hold values from 0 to 2047, as said below
- incidence: int32 [16, 16, 2048], P('src', 'tgt'), may hold values from 0 to 4095
- owner_map: int32 [16, 16], P('tgt'), may hold values from 0 to 15, each once within a row
- w_pre: bfloat16 [3, 512, 512], replicated, may hold values from -0.25 to 0.25
- w_post: bfloat16 [3, 512, 512], replicated, may hold values from -0.25 to 0.25
- w_out: bfloat16 [512, 256], replicated, may hold values from -0.125 to 0.125
Outputs:
- atom_messages: bfloat16 [16, 4096, 256], P('tgt', 'src')
Inputs may be any that keep to these rules, and one draw needn't show every extreme that they name: tile_counts[s, b] equals tile_counts[b, s]; some tile is full with 2048 live edges. For each tile (s, b), reverse_rows[s, b, :] is a permutation of the slots that maps live slots to live slots of tile (b, s). `owner_map`: each row is a permutation.
All inputs are finite; a program needn't handle non-finite values.
Results may differ from a plain program's by a relative error of at most 0.013.
Values may be sent and summed in bfloat16 or wider, within the bound.
A program may use at most 64 MiB of HBM per device.

v0:
```python
import jax
import jax.numpy as jnp
from jax import lax
from jax.sharding import Mesh
from jax.sharding import PartitionSpec as P

ATOMS_BLK = 4096
SRC = ("src_0", "src_1", "src_2")


HALF_ROOT = 0.7071067811865476


def cut_along(x, dim, devices):
    shape = x.shape
    parts = x.reshape(*shape[:dim], devices, shape[dim] // devices, *shape[dim + 1 :])
    return jnp.moveaxis(parts, dim, 0)


def sum_at_owner(x, axis, dim):
    devices = lax.axis_size(axis)
    parts = lax.all_to_all(cut_along(x, dim, devices), axis, 0, 0, tiled=True)
    return jnp.sum(parts, axis=0)


def sum_by_axis(x, axes, dim):
    far, near = axes
    own = sum_at_owner(cut_along(x, dim, lax.axis_size(far)), near, dim + 1)
    return jnp.sum(lax.all_to_all(own, far, 0, 0, tiled=True), axis=0)


def residual_stack(hidden, weights):
    for layer_index in range(weights.shape[0]):
        projected_edges = jnp.dot(hidden, weights[layer_index], preferred_element_type=jnp.float32)
        hidden = ((hidden.astype(jnp.float32) + jax.nn.silu(projected_edges)) * HALF_ROOT).astype(
            jnp.bfloat16
        )
    return hidden


def mirror_tiles(own_tiles):
    blocks, tile_capacity, feature_width = own_tiles.shape
    sources = lax.axis_size(SRC)
    piece_rows = tile_capacity // sources
    sectioned = lax.all_to_all(
        lax.all_to_all(
            own_tiles.reshape(1, blocks, sources, piece_rows, feature_width),
            SRC,
            split_axis=2,
            concat_axis=2,
            tiled=True,
        ),
        "tgt",
        split_axis=2,
        concat_axis=0,
        tiled=True,
    )
    landed = lax.all_to_all(sectioned, SRC, split_axis=0, concat_axis=2, tiled=True)
    return landed.reshape(blocks, tile_capacity, feature_width)


def shards(edge_feat, tile_counts, reverse_rows, incidence, owner_map, w_pre, w_post, w_out):
    own_tiles = edge_feat[0]
    blocks, tile_capacity, feature_width = own_tiles.shape
    first_pass = residual_stack(
        own_tiles.reshape(blocks * tile_capacity, feature_width), w_pre
    ).reshape(blocks, tile_capacity, feature_width)
    mirrored = mirror_tiles(first_pass)
    pulled = jax.vmap(lambda one_tile, ordering: one_tile[ordering])(mirrored, reverse_rows[0])
    joined = ((first_pass.astype(jnp.float32) + pulled.astype(jnp.float32)) * HALF_ROOT).astype(
        jnp.bfloat16
    )
    second_pass = residual_stack(joined.reshape(blocks * tile_capacity, feature_width), w_post)
    atom_message = jnp.dot(second_pass, w_out, preferred_element_type=jnp.float32).astype(
        jnp.bfloat16
    )
    slot_ids = lax.broadcasted_iota(jnp.int32, (blocks, tile_capacity), 1)
    block_ids = lax.broadcasted_iota(jnp.int32, (blocks, tile_capacity), 0)
    live_rows = slot_ids < tile_counts[0][:, None]
    target_rows = jnp.where(live_rows, block_ids * ATOMS_BLK + incidence[0], -1)
    sources = lax.axis_size(SRC)
    sub_rows = blocks * ATOMS_BLK // sources
    owners = owner_map[0]
    positions = lax.iota(jnp.int32, sub_rows * lax.axis_size(SRC))
    slot_of = positions // sub_rows
    matches = (owners[None, :] == slot_of[:, None]).astype(jnp.int32)
    chosen = jnp.sum(matches * lax.iota(jnp.int32, sources)[None, :], axis=1)
    group_rows = chosen * sub_rows + positions % sub_rows
    selector = (group_rows[:, None] == target_rows).astype(jnp.bfloat16)
    block_summed = sum_by_axis(
        jnp.dot(selector, atom_message, preferred_element_type=jnp.float32),
        (("src_0", "src_1"), "src_2"),
        0,
    )
    return block_summed.astype(jnp.bfloat16)[None]


def solution(mesh):
    finer = Mesh(
        mesh.devices.reshape(4, 2, 2, mesh.shape["tgt"]), ("src_0", "src_1", "src_2", "tgt")
    )
    return jax.shard_map(
        shards,
        mesh=finer,
        in_specs=(
            P(SRC, "tgt", None, None),
            P(SRC, "tgt"),
            P(SRC, "tgt", None),
            P(SRC, "tgt", None),
            P("tgt", None),
            P(),
            P(),
            P(),
        ),
        out_specs=P("tgt", SRC, None),
        check_vma=False,
    )
```

profile of v0, /device:TPU:1, one launch (start us, length us, event | category | flops | bytes accessed | tf_op | source)
XLA Modules:
  0.0 231.2 jit_solution(821151267214470714)
XLA Ops:
  0.0 0.0 copy-start
  0.0 4.5 %multiply_convert_fusion.5 = bf16[2048,512]{1,0:T(8,128)(2,1)S(1)} fusion(bf16[1,1,2048,512]{3,2,1,0:T(8,128)(2,1)} %param.8, bf16[3,512,512]{2,1,0:T(8,128)(2,1)} %param.13), kind=kOutput, calls=%fused_computation.14 | convolution fusion | flops 1082130432 | bytes 6815744 | tf_op jit(solution)/shard_map/dot_general | solution.py:34
  4.5 0.0 copy-done.2
  4.5 1.3 fusion.25
  5.8 3.9 %multiply_convert_fusion.3 = bf16[2048,512]{1,0:T(8,128)(2,1)S(1)} fusion(f32[2048,512]{1,0:T(8,128)S(1)} %fusion.25, bf16[2048,512]{1,0:T(8,128)(2,1)S(1)} %multiply_convert_fusion.5, bf16[3,512,512]{2,1,0:T(8,128)(2,1)S(1)} %copy-done.2), kind=kOutput, calls=%fused_computation.12 | convolution fusion | flops 1098907648 | bytes 15204352 | tf_op jit(solution)/shard_map/dot_general | solution.py:34
  9.7 0.0 copy-start.1
  9.7 36.4 %all_to_all.36 = bf16[1,1,16,128,512]{4,3,1,0,2:T(8,128)(2,1)S(1)} all-to-all(bf16[1,1,16,128,512]{4,3,1,0,2:T(8,128)(2,1)S(1)} %bitcast.60), channel_id=1, replica_groups=mesh['src_0'=4,'src_1'=2,'src_2'=2,'tgt'=16] {'src_0','src_1','src_2'}, dimensions={2} | all-to-all | bytes 4194304 | tf_op jit(solution)/shard_map/all_to_all | solution.py:46
  46.1 57.5 %all_to_all.37 = bf16[1,1,16,128,512]{4,3,1,0,2:T(8,128)(2,1)} all-to-all(bf16[1,1,16,128,512]{4,3,1,0,2:T(8,128)(2,1)S(1)} %all_to_all.36), channel_id=1, replica_groups=mesh['src_0'=4,'src_1'=2,'src_2'=2,'tgt'=16] {'tgt'}, dimensions={2} | all-to-all | bytes 4194304 | tf_op jit(solution)/shard_map/all_to_all | solution.py:45
  103.6 0.0 copy-done.1
  103.6 7.1 %all-to-all-start.2 = ((bf16[16,1,1,128,512]{4,3,2,1,0:T(8,128)(2,1)}), bf16[16,1,1,128,512]{4,3,2,1,0:T(8,128)(2,1)S(1)}, u32[]{:S(2)}, u32[]{:S(2)}) async-start(bf16[16,1,1,128,512]{4,3,2,1,0:T(8,128)(2,1)} %bitcast.58), calls=%async_computation.2 | async-start | bytes 4194304 | tf_op jit(solution)/shard_map/all_to_all | solution.py:58
  111.3 0.0 copy-done.6
  111.3 0.1 select_reduce_fusion
  111.5 0.0 copy-done.5
  111.6 27.6 %all-to-all-done.2 = bf16[16,1,1,128,512]{4,3,2,1,0:T(8,128)(2,1)S(1)} async-done(((bf16[16,1,1,128,512]{4,3,2,1,0:T(8,128)(2,1)}), bf16[16,1,1,128,512]{4,3,2,1,0:T(8,128)(2,1)S(1)}, u32[]{:S(2)}, u32[]{:S(2)}) %all-to-all-start.2) | async-done | bytes 2097184 | tf_op jit(solution)/shard_map/all_to_all | solution.py:58
  139.1 21.7 %gather_fusion = bf16[2048,512]{1,0:T(8,128)(2,1)} fusion(bf16[1,2048,512]{2,1,0:T(8,128)(2,1)S(1)} %bitcast.55, s32[2048]{0:T(1024)S(1)} %bitcast.56), kind=kCustom, calls=%fused_computation | custom fusion | bytes 4210688 | tf_op jit(solution)/shard_map/vmap()/gather | solution.py:69
  160.8 6.3 %multiply_convert_fusion.2 = bf16[2048,512]{1,0:T(8,128)(2,1)S(1)} fusion(bf16[2048,512]{1,0:T(8,128)(2,1)} %gather_fusion, bf16[2048,512]{1,0:T(8,128)(2,1)} %copy-done.1, bf16[3,512,512]{2,1,0:T(8,128)(2,1)} %param.14), kind=kOutput, calls=%fused_computation.11 | convolution fusion | flops 1092616192 | bytes 11010048 | tf_op jit(solution)/shard_map/dot_general | solution.py:34
  167.1 2.0 multiply_convert_fusion.1
  169.1 3.2 %fusion.14 = f32[2048,512]{1,0:T(8,128)} fusion(bf16[2048,512]{1,0:T(8,128)(2,1)S(1)} %multiply_convert_fusion.1, bf16[3,512,512]{2,1,0:T(8,128)(2,1)S(1)} %copy-done.3), kind=kOutput, calls=%fused_computation.19 | convolution fusion | flops 1073741824 | bytes 6815744 | tf_op jit(solution)/shard_map/dot_general | solution.py:34
  172.3 11.0 %fusion = f32[4096,256]{1,0:T(8,128)} fusion(s32[2048]{0:T(1024)S(1)} %fusion.45, s32[4096]{0:T(1024)S(1)} %fusion.40, bf16[512,256]{1,0:T(8,128)(2,1)S(1)} %copy-done, f32[2048,512]{1,0:T(8,128)} %fusion.14, bf16[2048,512]{1,0:T(8,128)(2,1)S(1)} %multiply_convert_fusion.1), kind=kOutput, calls=%fused_computation.1 | convolution fusion | flops 4849139712 | bytes 10772480 | tf_op jit(solution)/shard_map/dot_general | solution.py:91
  183.3 2.6 %copy.16 = f32[8,2,256,256]{3,2,0,1:T(8,128)S(1)} copy(f32[8,2,256,256]{3,2,1,0:T(8,128)} %bitcast.59) | data formatting | bytes 8388608 | tf_op jit(solution)/shard_map/reshape;reshape | solution.py:16
  185.9 8.7 %all_to_all.38 = f32[2,8,256,256]{3,2,1,0:T(8,128)} all-to-all(f32[2,8,256,256]{3,2,1,0:T(8,128)S(1)} %bitcast.57), channel_id=1, replica_groups=mesh['src_0'=4,'src_1'=2,'src_2'=2,'tgt'=16] {'src_2'}, dimensions={0} | all-to-all | bytes 8388608 | tf_op jit(solution)/shard_map/all_to_all | solution.py:22
  194.6 2.7 %reduce_sum.28 = f32[8,256,256]{2,1,0:T(8,128)S(1)} reduce(f32[2,8,256,256]{3,2,1,0:T(8,128)} %all_to_all.38, f32[]{:T(128)} %constant.50.clone.1), dimensions={0}, to_apply=%region_1.2 | reduce | flops 524288 | bytes 6291460 | tf_op jit(solution)/shard_map/reduce_sum | solution.py:23
  197.4 31.4 %all_to_all.39 = f32[8,256,256]{2,1,0:T(8,128)} all-to-all(f32[8,256,256]{2,1,0:T(8,128)S(1)} %reduce_sum.28), channel_id=1, replica_groups=mesh['src_0'=4,'src_1'=2,'src_2'=2,'tgt'=16] {'src_0','src_1'}, dimensions={0} | all-to-all | bytes 4194304 | tf_op jit(solution)/shard_map/all_to_all | solution.py:29
  228.7 2.4 %reduce_sum.29 = bf16[256,256]{1,0:T(8,128)(2,1)} reduce(f32[8,256,256]{2,1,0:T(8,128)} %all_to_all.39, f32[]{:T(128)} %constant.50.clone.1), dimensions={0}, to_apply=%region_2.3 | reduce | flops 458752 | bytes 2228228 | tf_op jit(solution)/shard_map/reduce_sum | solution.py:29
  (14 shorter events, 0.1 us)
Async XLA Ops:
  0.0 172.3 %copy-start = (bf16[512,256]{1,0:T(8,128)(2,1)S(1)}, bf16[512,256]{1,0:T(8,128)(2,1)}, u32[]{:S(2)}) copy-start(bf16[512,256]{1,0:T(8,128)(2,1)} %param.15) | copy-start | bytes 786436
  0.0 4.5 %copy-start.2 = (bf16[3,512,512]{2,1,0:T(8,128)(2,1)S(1)}, bf16[3,512,512]{2,1,0:T(8,128)(2,1)}, u32[]{:S(2)}) copy-start(bf16[3,512,512]{2,1,0:T(8,128)(2,1)} %param.13) | copy-start | bytes 4718596
  9.7 93.9 %copy-start.1 = (bf16[2048,512]{1,0:T(8,128)(2,1)}, bf16[2048,512]{1,0:T(8,128)(2,1)S(1)}, u32[]{:S(2)}) copy-start(bf16[2048,512]{1,0:T(8,128)(2,1)S(1)} %multiply_convert_fusion.3) | copy-start | bytes 6291460
  46.1 65.3 %copy-start.6 = (s32[1,16]{1,0:T(1,128)S(1)}, s32[1,16]{1,0:T(1,128)}, u32[]{:S(2)}) copy-start(s32[1,16]{1,0:T(1,128)} %param.12) | copy-start | bytes 196
  46.1 65.4 %copy-start.4 = (s32[1,1,2048]{2,1,0:T(1,128)S(1)}, s32[1,1,2048]{2,1,0:T(1,128)}, u32[]{:S(2)}) copy-start(s32[1,1,2048]{2,1,0:T(1,128)} %param.10) | copy-start | bytes 24580
  46.1 65.4 %copy-start.5 = (s32[1,1,2048]{2,1,0:T(1,128)S(1)}, s32[1,1,2048]{2,1,0:T(1,128)}, u32[]{:S(2)}) copy-start(s32[1,1,2048]{2,1,0:T(1,128)} %param.11) | copy-start | bytes 24580
  103.6 35.5 %all-to-all-start.2 = ((bf16[16,1,1,128,512]{4,3,2,1,0:T(8,128)(2,1)}), bf16[16,1,1,128,512]{4,3,2,1,0:T(8,128)(2,1)S(1)}, u32[]{:S(2)}, u32[]{:S(2)}) async-start(bf16[16,1,1,128,512]{4,3,2,1,0:T(8,128)(2,1)} %bitcast.58), calls=%async_computation.2 | async-start | bytes 4194304 | tf_op jit(solution)/shard_map/all_to_all | solution.py:58
  160.8 6.3 %copy-start.3 = (bf16[3,512,512]{2,1,0:T(8,128)(2,1)S(1)}, bf16[3,512,512]{2,1,0:T(8,128)(2,1)}, u32[]{:S(2)}) copy-start(bf16[3,512,512]{2,1,0:T(8,128)(2,1)} %param.14) | copy-start | bytes 4718596
where the time goes:
time: 232 us; the launch traced here: 231 us
  blocking collectives  134 us (58%)
  matrix products  32.1 us (14%)
  waiting for transfers between devices  27.6 us (12%)
  local copies, waits for them, and re-layouts  24.3 us (10%)
  starting transfers between devices  7.07 us (3%)
  other arithmetic  5.33 us (2%)
    all_to_all x1, blocking collectives, mirror_tiles(): lax.all_to_all(lax.all_to_all(own_tiles.reshape(1, blocks, sources, piece...  57.5 us
    all_to_all x1, blocking collectives, mirror_tiles(): lax.all_to_all(own_tiles.reshape(1, blocks, sources, piece_rows, feature_...  36.4 us
    all_to_all x1, blocking collectives, sum_by_axis(): return jnp.sum(lax.all_to_all(own, far, 0, 0, tiled=True), axis=0)  31.4 us
    all_to_all x1, waiting for transfers between devices, mirror_tiles(): lax.all_to_all(sectioned, SRC, split_axis=0, concat_axis=2, tiled=True)  27.6 us
    gather x2, local copies, waits for them, and re-layouts, shards(): one_tile[ordering]  21.7 us
    dot_general x6, matrix products, residual_stack(): jnp.dot(hidden, weights[layer_index], preferred_element_type=jnp.float32)  21.1 us
    dot_general x1, matrix products, shards(): jnp.dot(selector, atom_message, preferred_element_type=jnp.float32)  11 us
    all_to_all x1, blocking collectives, sum_at_owner(): parts = lax.all_to_all(cut_along(x, dim, devices), axis, 0, 0, tiled=True)  8.73 us
  transfers between devices with their start and end apart: 1, of which 1 were waited for; matrix products, arithmetic and copies ran while one was open for 0% of the time, Pallas kernels for 0%

commit v1 on v0

v1 whole, which is shorter than its diff:
```python
import jax
import jax.numpy as jnp
from jax import lax
from jax.experimental import pallas as pl
from jax.experimental.pallas import tpu as pltpu
from jax.sharding import Mesh
from jax.sharding import PartitionSpec as P

SUB = 256
HALF_ROOT = 0.7071067811865476
MESH = pl.DeviceIdType.MESH
SRC = ("y", "xh", "c")
TGT = ("z", "xl")
CHUNKS = 8
LAG = 2
F32 = jnp.float32
BF16 = jnp.bfloat16


def layer(hidden, weight):
    half = jnp.dot(hidden, weight, preferred_element_type=F32) * 0.5
    silu = half + half * jnp.tanh(half)
    return ((hidden.astype(F32) + silu) * HALF_ROOT).astype(BF16)


def where_am_i():
    return tuple(lax.axis_index(name) for name in ("y", "xh", "c", "z", "xl"))


def mirror_kernel(
    edge_ref, w_ref, rev_ref, joined_ref,
    first, spread, moved, landed, total, rev_wide,
    send1, recv1, send2, recv2, send3, recv3,
):
    y, xh, c, z, xl = where_am_i()
    zy, z0 = z // 2, lax.rem(z, 2)
    alone = (xh == z0) & (xl == c)
    rows, width = edge_ref.shape
    chunk = rows // CHUNKS
    piece = chunk // 4

    def beside(step):
        return (lax.rem(y + step, 4), xh, c, z, xl)

    def across(step):
        return (y, z0, xl, 2 * lax.rem(zy + step, 4) + xh, c)

    barrier = pltpu.get_barrier_semaphore()
    for step in range(1, 4):
        pl.semaphore_signal(barrier, inc=1, device_id=beside(step), device_id_type=MESH)
        pl.semaphore_signal(barrier, inc=1, device_id=across(step), device_id_type=MESH)

    @pl.when(jnp.logical_not(alone))
    def _():
        pl.semaphore_signal(barrier, inc=1, device_id=across(0), device_id_type=MESH)

    def remote(src, dst, send, recv, device):
        return pltpu.make_async_remote_copy(
            src_ref=src, dst_ref=dst, send_sem=send, recv_sem=recv,
            device_id=device, device_id_type=MESH,
        )

    def copy1(g, step):
        start = pl.multiple_of(g * chunk + lax.rem(y + step, 4) * piece, piece)
        return remote(
            first.at[pl.ds(start, piece)], spread.at[g, step],
            send1.at[g, step], recv1.at[g, step], beside(step),
        )

    def copy2(g, step):
        held = lax.rem(y - zy - step + 8, 4)
        return remote(
            spread.at[g, held], moved.at[g, step],
            send2.at[g, step], recv2.at[g, step], across(step),
        )

    def stay2(g):
        held = lax.rem(y - zy + 8, 4)
        return pltpu.make_async_copy(spread.at[g, held], moved.at[g, 0], recv2.at[g, 0])

    def copy3(g, step):
        held = lax.rem(zy - y - step + 8, 4)
        return remote(
            moved.at[g, held], landed.at[g, step],
            send3.at[g, step], recv3.at[g, step], beside(step),
        )

    def embed(g):
        here = pl.ds(pl.multiple_of(g * chunk, chunk), chunk)
        hidden = edge_ref[here, :]
        for index in range(w_ref.shape[0]):
            hidden = layer(hidden, w_ref[index])
        first[here, :] = hidden

    def stage(i, carry):
        @pl.when(i < CHUNKS)
        def _():
            for step in range(1, 4):
                copy1(i, step).start()
            own = pl.ds(pl.multiple_of(i * chunk + y * piece, piece), piece)
            spread[i, 0] = first[own, :]

        @pl.when(i + 1 < CHUNKS)
        def _():
            embed(i + 1)

        @pl.when((i >= 1) & (i <= CHUNKS))
        def _():
            g = i - 1
            for step in range(1, 4):
                copy1(g, step).wait_recv()
            for step in range(1, 4):
                copy2(g, step).start()

            @pl.when(alone)
            def _():
                stay2(g).start()

            @pl.when(jnp.logical_not(alone))
            def _():
                copy2(g, 0).start()

        @pl.when((i >= 1 + LAG) & (i <= CHUNKS + LAG))
        def _():
            g = i - 1 - LAG
            for step in range(1, 4):
                copy2(g, step).wait_recv()

            @pl.when(alone)
            def _():
                stay2(g).wait()

            @pl.when(jnp.logical_not(alone))
            def _():
                copy2(g, 0).wait_recv()

            for step in range(1, 4):
                copy3(g, step).start()
            landed[g, 0] = moved[g, lax.rem(zy - y + 4, 4)]

        @pl.when(i == 1 + LAG)
        def _():
            total[...] = jnp.zeros_like(total)

        @pl.when(i >= 2 + LAG)
        def _():
            g = i - 2 - LAG
            for step in range(1, 4):
                copy3(g, step).wait_recv()
            block = landed[g].reshape(chunk, width)
            lane = lax.broadcasted_iota(jnp.int32, (1, chunk), 1)
            slot, offset = lane // piece, lane % piece
            origin = g * chunk + ((y + 4 - slot) % 4) * piece + offset

            def add(t, carry):
                some = pl.ds(pl.multiple_of(t * 256, 256), 256)
                picked = jnp.concatenate([rev_wide[some, :]] * (chunk // 128), axis=1)
                choose = jnp.where(picked == origin, 1.0, 0.0).astype(BF16)
                total[some, :] += jnp.dot(choose, block, preferred_element_type=F32)
                return carry

            lax.fori_loop(0, rows // 256, add, 0)

        return carry

    embed(0)

    def widen(t, carry):
        part = pl.ds(pl.multiple_of(t * 128, 128), 128)
        rev_wide[part, :] = jnp.broadcast_to(rev_ref[:, part], (128, 128)).T
        return carry

    lax.fori_loop(0, rows // 128, widen, 0)

    pl.semaphore_wait(barrier, jnp.where(alone, 6, 7))
    lax.fori_loop(0, CHUNKS + LAG + 2, stage, 0)

    def finish(g, carry):
        here = pl.ds(pl.multiple_of(g * chunk, chunk), chunk)
        both = first[here, :].astype(F32) + total[here, :]
        joined_ref[here, :] = (both * HALF_ROOT).astype(BF16)
        for step in range(1, 4):
            copy1(g, step).wait_send()
            copy2(g, step).wait_send()
            copy3(g, step).wait_send()

        @pl.when(jnp.logical_not(alone))
        def _():
            copy2(g, 0).wait_send()

        return carry

    lax.fori_loop(0, CHUNKS, finish, 0)


def mirror(edge, w_pre, rev):
    rows, width = edge.shape
    piece = rows // CHUNKS // 4
    pieces = pltpu.VMEM((CHUNKS, 4, piece, width), BF16)
    sems = pltpu.SemaphoreType.DMA((CHUNKS, 4))
    vmem = pl.BlockSpec(memory_space=pltpu.VMEM)
    return pl.pallas_call(
        mirror_kernel,
        name="mirror",
        out_shape=jax.ShapeDtypeStruct((rows, width), BF16),
        in_specs=[vmem] * 3,
        out_specs=vmem,
        scratch_shapes=[
            pltpu.VMEM((rows, width), BF16),
            pieces, pieces, pieces,
            pltpu.VMEM((rows, width), F32),
            pltpu.VMEM((rows, 128), jnp.int32),
            sems, sems, sems, sems, sems, sems,
        ],
        compiler_params=pltpu.CompilerParams(
            collective_id=0, has_side_effects=True, vmem_limit_bytes=40 << 20
        ),
    )(edge, w_pre, rev)


def message_kernel(joined_ref, w_ref, w_out_ref, message_ref):
    hidden = joined_ref[...]
    for index in range(w_ref.shape[0]):
        hidden = layer(hidden, w_ref[index])
    message_ref[...] = jnp.dot(hidden, w_out_ref[...], preferred_element_type=F32).astype(BF16)


def messages(joined, w_post, w_out):
    rows, width = joined.shape
    tile = 512
    return pl.pallas_call(
        message_kernel,
        name="messages",
        grid=(rows // tile,),
        out_shape=jax.ShapeDtypeStruct((rows, w_out.shape[1]), BF16),
        in_specs=[
            pl.BlockSpec((tile, width), lambda i: (i, 0)),
            pl.BlockSpec(w_post.shape, lambda i: (0, 0, 0)),
            pl.BlockSpec(w_out.shape, lambda i: (0, 0)),
        ],
        out_specs=pl.BlockSpec((tile, w_out.shape[1]), lambda i: (i, 0)),
        compiler_params=pltpu.CompilerParams(vmem_limit_bytes=24 << 20),
    )(joined, w_post, w_out)


HOPS = ((2, 1), (1, 1), (3, 1), (2, 0), (0, 1), (1, 0), (3, 0), (0, 0))


def reduce_kernel(
    message_ref, atom_ref, count_ref, owner_ref, out_ref,
    target, mine, pair_out, pair_in, far_out, far_in,
    pair_send, pair_recv, far_send, far_recv,
):
    y, xh, c, z, xl = where_am_i()
    edges, width = message_ref.shape
    other = (y, xh, 1 - c, z, xl)

    def owner_of(hop):
        return lax.rem(y + HOPS[hop][0], 4), lax.rem(xh + HOPS[hop][1], 2)

    def far_device(hop):
        return (*owner_of(hop), c, z, xl)

    barrier = pltpu.get_barrier_semaphore()
    pl.semaphore_signal(barrier, inc=1, device_id=other, device_id_type=MESH)
    for hop in range(7):
        pl.semaphore_signal(barrier, inc=1, device_id=far_device(hop), device_id_type=MESH)

    atoms = atom_ref[...]
    block = atoms // SUB
    place = jnp.zeros_like(atoms)
    for k in range(owner_ref.shape[1]):
        place = jnp.where(block == k, owner_ref[0, k], place)
    slot = lax.broadcasted_iota(jnp.int32, atoms.shape, 1)
    target[...] = jnp.where(slot < count_ref[0, 0], place * SUB + atoms % SUB, -1)
    pl.semaphore_wait(barrier, 8)

    row = lax.broadcasted_iota(jnp.int32, (SUB, edges), 0)

    def part(position):
        select = jnp.where(row == target[...] - position * SUB, 1.0, 0.0).astype(BF16)
        return jnp.dot(select, message_ref[...], preferred_element_type=F32)

    def pair_copy(hop):
        return pltpu.make_async_remote_copy(
            src_ref=pair_out.at[hop], dst_ref=pair_in.at[hop],
            send_sem=pair_send.at[hop], recv_sem=pair_recv.at[hop],
            device_id=other, device_id_type=MESH,
        )

    def far_copy(hop):
        return pltpu.make_async_remote_copy(
            src_ref=far_out.at[hop], dst_ref=far_in.at[hop],
            send_sem=far_send.at[hop], recv_sem=far_recv.at[hop],
            device_id=far_device(hop), device_id_type=MESH,
        )

    def send_on(hop):
        pair_copy(hop).wait_recv()
        chip_sum = mine[hop % 2] + pair_in[hop].astype(F32)
        if hop < 7:
            far_out[hop] = chip_sum.astype(BF16)
            far_copy(hop).start()
            return None
        return chip_sum

    for hop in range(8):
        to_y, to_xh = owner_of(hop)
        position = 4 * to_y + 2 * to_xh
        pair_out[hop] = part(position + 1 - c).astype(BF16)
        pair_copy(hop).start()
        mine[hop % 2] = part(position + c)
        if hop > 0:
            send_on(hop - 1)
    result = send_on(7)
    for hop in range(7):
        far_copy(hop).wait_recv()
        result = result + far_in[hop].astype(F32)
    out_ref[...] = result.astype(BF16)
    for hop in range(8):
        pair_copy(hop).wait_send()
    for hop in range(7):
        far_copy(hop).wait_send()


def reduce_to_owner(message, atoms, count, owners):
    width = message.shape[1]
    blocks = lambda n: pltpu.VMEM((n, SUB, width), BF16)
    sems = pltpu.SemaphoreType.DMA((8,))
    vmem = pl.BlockSpec(memory_space=pltpu.VMEM)
    smem = pl.BlockSpec(memory_space=pltpu.SMEM)
    return pl.pallas_call(
        reduce_kernel,
        name="reduce_to_owner",
        out_shape=jax.ShapeDtypeStruct((SUB, width), BF16),
        in_specs=[vmem, vmem, smem, smem],
        out_specs=vmem,
        scratch_shapes=[
            pltpu.VMEM(atoms.shape, jnp.int32),
            pltpu.VMEM((2, SUB, width), F32),
            blocks(8), blocks(8), blocks(7), blocks(7),
            sems, sems, sems, sems,
        ],
        compiler_params=pltpu.CompilerParams(
            collective_id=1, has_side_effects=True, vmem_limit_bytes=24 << 20
        ),
    )(message, atoms, count, owners)


def shards(edge_feat, tile_counts, reverse_rows, incidence, owner_map, w_pre, w_post, w_out):
    joined = mirror(edge_feat[0, 0], w_pre, reverse_rows[0])
    message = messages(joined, w_post, w_out)
    return reduce_to_owner(message, incidence[0], tile_counts, owner_map)[None]


def solution(mesh):
    finer = Mesh(mesh.devices.reshape(4, 2, 2, 8, 2), ("y", "xh", "c", "z", "xl"))
    return jax.shard_map(
        shards,
        mesh=finer,
        in_specs=(
            P(SRC, TGT, None, None),
            P(SRC, TGT),
            P(SRC, TGT, None),
            P(SRC, TGT, None),
            P(TGT, None),
            P(),
            P(),
            P(),
        ),
        out_specs=P(TGT, SRC, None),
        check_vma=False,
    )
```

time: 232 us -> 131 us (0.56)
  blocking collectives: 134 us -> 0 us
  Pallas kernels: 0 us -> 125 us
  matrix products: 32.1 us -> 0 us
  waiting for transfers between devices: 27.6 us -> 0 us
  local copies, waits for them, and re-layouts: 24.3 us -> 4.37 us
  starting transfers between devices: 7.07 us -> 0 us
  other arithmetic: 5.33 us -> 0 us
    all_to_all x4 -> x0, blocking collectives: 134 us -> none  [the longest x1 57.5 us: mirror_tiles(): lax.all_to_all(lax.all_to_all(own_tiles.reshape(1, blocks, sources, piece...]
    pallas_call x0 -> x3, Pallas kernels: none -> 125 us  [the longest x1 66.7 us: mirror(): pl.pallas_call(mirror_kernel, name='mirror', out_shape=jax.ShapeDtypeStru...]
    dot_general x7 -> x0, matrix products: 32.1 us -> none  [the longest x6 21.1 us: residual_stack(): jnp.dot(hidden, weights[layer_index], preferred_element_type=jnp.float32)]
    all_to_all x1 -> x0, waiting for transfers between devices: 27.6 us -> none  [mirror_tiles(): lax.all_to_all(sectioned, SRC, split_axis=0, concat_axis=2, tiled=True)]
    gather x2 -> x0, local copies, waits for them, and re-layouts: 21.7 us -> none  [shards(): one_tile[ordering]]
    all_to_all x1 -> x0, starting transfers between devices: 7.07 us -> none  [mirror_tiles(): lax.all_to_all(sectioned, SRC, split_axis=0, concat_axis=2, tiled=True)]
    reduce_sum x3 -> x0, other arithmetic: 5.27 us -> none  [the longest x1 2.73 us: sum_at_owner(): return jnp.sum(parts, axis=0)]
    unnamed x14 -> x15, local copies, waits for them, and re-layouts: 0.03 us -> 4.37 us
  transfers between devices with their start and end apart: 1 -> 0, of which waited for: 1 -> 0; matrix products, arithmetic and copies ran while one was open for 0% -> 0% of each run, Pallas kernels for 0% -> 0%
where the time goes in v1:
time: 131 us
  Pallas kernels  125 us (95%)
  local copies, waits for them, and re-layouts  4.37 us (3%)
    pallas_call x1, Pallas kernels, mirror(): pl.pallas_call(mirror_kernel, name='mirror', out_shape=jax.ShapeDtypeStru...  66.7 us
    pallas_call x1, Pallas kernels, reduce_to_owner(): pl.pallas_call(reduce_kernel, name='reduce_to_owner', out_shape=jax.Shape...  53.1 us
    pallas_call x1, Pallas kernels, messages(): pl.pallas_call(message_kernel, name='messages', grid=(rows // tile,), out...  5.59 us
    unnamed x15, local copies, waits for them, and re-layouts  4.37 us

profile of v1, /device:TPU:1, one launch (start us, length us, event | category | flops | bytes accessed | tf_op | source)
XLA Modules:
  0.0 130.5 jit_solution(1059246801531162858)
XLA Ops:
  0.0 0.0 copy-start
  0.0 1.6 %copy-done = bf16[1,1,2048,512]{3,2,1,0:T(8,128)(2,1)S(1)} copy-done((bf16[1,1,2048,512]{3,2,1,0:T(8,128)(2,1)S(1)}, bf16[1,1,2048,512]{3,2,1,0:T(8,128)(2,1)}, u32[]{:S(2)}) %copy-start) | copy-done | bytes 2097176
  1.6 0.0 copy-start.2
  1.6 1.4 %copy-done.2 = bf16[3,512,512]{2,1,0:T(8,128)(2,1)S(1)} copy-done((bf16[3,512,512]{2,1,0:T(8,128)(2,1)S(1)}, bf16[3,512,512]{2,1,0:T(8,128)(2,1)}, u32[]{:S(2)}) %copy-start.2) | copy-done | bytes 1572888
  3.0 0.0 copy-start.4
  3.0 0.7 copy-done.4
  3.7 0.0 copy-start.1
  3.7 0.0 copy-start.3
  3.7 66.7 %mirror.1.joined_ref = bf16[2048,512]{1,0:T(8,128)(2,1)S(1)} custom-call(bf16[2048,512]{1,0:T(8,128)(2,1)S(1)} %bitcast.4, bf16[3,512,512]{2,1,0:T(8,128)(2,1)S(1)} %copy-done.2, s32[1,2048]{1,0:T(1,128)S(1)} %bitcast.6), custom_call_target="tpu_custom_call" | custom-call | tf_op jit(solution)/shard_map/mirror/pallas_call | solution.py:202
  70.4 0.0 copy-done.1
  70.4 0.0 copy-done.3
  70.4 0.0 copy-start.5
  70.4 0.0 copy-start.6
  70.5 5.6 %messages.1.message_ref = bf16[2048,256]{1,0:T(8,128)(2,1)S(1)} custom-call(bf16[2048,512]{1,0:T(8,128)(2,1)S(1)} %mirror.1.joined_ref, bf16[3,512,512]{2,1,0:T(8,128)(2,1)S(1)} %copy-done.1, bf16[512,256]{1,0:T(8,128)(2,1)S(1)} %copy-done.3), custom_call_target="tpu_custom_call" | custom-call | tf_op jit(solution)/shard_map/messages/pallas_call | solution.py:231
  76.7 0.0 copy-done.5
  76.7 0.0 copy-done.6
  76.7 53.1 %reduce_to_owner.1 = bf16[256,256]{1,0:T(8,128)(2,1)S(1)} custom-call(bf16[2048,256]{1,0:T(8,128)(2,1)S(1)} %messages.1.message_ref, s32[1,2048]{1,0:T(1,128)S(1)} %bitcast.7, s32[1,1]{1,0:T(1,128)S(6)} %copy.10.count_ref, s32[1,16]{1,0:T(1,128)S(1)} %copy-done.6), custom_call_target="tpu_custom_call" | custom-call | tf_op jit(solution)/shard_map/reduce_to_owner/pallas_call | solution.py:332
  129.9 0.7 copy.11
Async XLA Ops:
  0.0 1.6 %copy-start = (bf16[1,1,2048,512]{3,2,1,0:T(8,128)(2,1)S(1)}, bf16[1,1,2048,512]{3,2,1,0:T(8,128)(2,1)}, u32[]{:S(2)}) copy-start(bf16[1,1,2048,512]{3,2,1,0:T(8,128)(2,1)} %param.8) | copy-start | bytes 6291460
  1.6 1.4 %copy-start.2 = (bf16[3,512,512]{2,1,0:T(8,128)(2,1)S(1)}, bf16[3,512,512]{2,1,0:T(8,128)(2,1)}, u32[]{:S(2)}) copy-start(bf16[3,512,512]{2,1,0:T(8,128)(2,1)} %w_ref.2) | copy-start | bytes 4718596
  3.0 0.7 copy-start.4
  3.7 66.7 %copy-start.1 = (bf16[3,512,512]{2,1,0:T(8,128)(2,1)S(1)}, bf16[3,512,512]{2,1,0:T(8,128)(2,1)}, u32[]{:S(2)}) copy-start(bf16[3,512,512]{2,1,0:T(8,128)(2,1)} %w_ref.3) | copy-start | bytes 4718596
  3.7 66.7 %copy-start.3 = (bf16[512,256]{1,0:T(8,128)(2,1)S(1)}, bf16[512,256]{1,0:T(8,128)(2,1)}, u32[]{:S(2)}) copy-start(bf16[512,256]{1,0:T(8,128)(2,1)} %w_out_ref.1) | copy-start | bytes 786436
  70.4 6.3 %copy-start.5 = (s32[1,1,2048]{2,1,0:T(1,128)S(1)}, s32[1,1,2048]{2,1,0:T(1,128)}, u32[]{:S(2)}) copy-start(s32[1,1,2048]{2,1,0:T(1,128)} %param.11) | copy-start | bytes 24580
  70.4 6.3 %copy-start.6 = (s32[1,16]{1,0:T(1,128)S(1)}, s32[1,16]{1,0:T(1,128)}, u32[]{:S(2)}) copy-start(s32[1,16]{1,0:T(1,128)} %owner_ref.1) | copy-start | bytes 196

commit v2 on v1

--- a/solution.py
+++ b/solution.py
@@ -29,30 +29,43 @@
 
 def mirror_kernel(
     edge_ref, w_ref, rev_ref, joined_ref,
-    first, spread, moved, landed, total, rev_wide,
-    send1, recv1, send2, recv2, send3, recv3,
+    first, spread, midway, moved, landed, total, rev_wide,
+    send1, recv1, send2, recv2, send3, recv3, send4, recv4,
 ):
     y, xh, c, z, xl = where_am_i()
     zy, z0 = z // 2, lax.rem(z, 2)
-    alone = (xh == z0) & (xl == c)
+    odd = lax.rem(xh + z0, 2)
+    relay = odd == 0
+    settled = c == xl
+    alone = relay & settled
+    far = jnp.logical_not(alone)
+    leaf = jnp.logical_not(relay)
     rows, width = edge_ref.shape
     chunk = rows // CHUNKS
     piece = chunk // 4
 
-    def beside(step):
+    def along_y(step):
         return (lax.rem(y + step, 4), xh, c, z, xl)
 
-    def across(step):
-        return (y, z0, xl, 2 * lax.rem(zy + step, 4) + xh, c)
+    def along_z(step):
+        return (y, xh, c, lax.rem(z + step, 8), xl)
+
+    def along_x(flip):
+        return (y, lax.rem(xh + flip, 2), xl, z, c)
+
+    def greet(device):
+        pl.semaphore_signal(barrier, inc=1, device_id=device, device_id_type=MESH)
 
     barrier = pltpu.get_barrier_semaphore()
     for step in range(1, 4):
-        pl.semaphore_signal(barrier, inc=1, device_id=beside(step), device_id_type=MESH)
-        pl.semaphore_signal(barrier, inc=1, device_id=across(step), device_id_type=MESH)
-
-    @pl.when(jnp.logical_not(alone))
+        greet(along_y(step))
+    for step in range(1, 8):
+        greet(along_z(step))
+    greet(along_x(1))
+
+    @pl.when(jnp.logical_not(settled))
     def _():
-        pl.semaphore_signal(barrier, inc=1, device_id=across(0), device_id_type=MESH)
+        greet(along_x(0))
 
     def remote(src, dst, send, recv, device):
         return pltpu.make_async_remote_copy(
@@ -60,29 +73,74 @@
             device_id=device, device_id_type=MESH,
         )
 
+    def when(condition, work):
+        if condition is True:
+            work()
+        else:
+            pl.when(condition)(work)
+
     def copy1(g, step):
         start = pl.multiple_of(g * chunk + lax.rem(y + step, 4) * piece, piece)
         return remote(
             first.at[pl.ds(start, piece)], spread.at[g, step],
-            send1.at[g, step], recv1.at[g, step], beside(step),
-        )
-
-    def copy2(g, step):
-        held = lax.rem(y - zy - step + 8, 4)
-        return remote(
-            spread.at[g, held], moved.at[g, step],
-            send2.at[g, step], recv2.at[g, step], across(step),
-        )
-
-    def stay2(g):
-        held = lax.rem(y - zy + 8, 4)
-        return pltpu.make_async_copy(spread.at[g, held], moved.at[g, 0], recv2.at[g, 0])
-
-    def copy3(g, step):
+            send1.at[g, step], recv1.at[g, step], along_y(step),
+        )
+
+    def hop2(m):
+        return 2 * m + odd
+
+    def held2(m):
+        return lax.rem(y + 8 - lax.rem(z + hop2(m), 8) // 2, 4)
+
+    def copy2(x_first, g, m):
+        return remote(
+            spread.at[g, held2(m)], midway.at[g, hop2(m)],
+            send2.at[g, m], recv2.at[g, hop2(m)],
+            along_x(odd) if x_first else along_z(hop2(m)),
+        )
+
+    def far2(x_first, m):
+        return far if x_first else (leaf if m == 0 else True)
+
+    def near2(x_first, m):
+        return alone if x_first else (relay if m == 0 else False)
+
+    def slot3(x_first, hop):
+        turn = z0 if x_first else 1 - z0
+        return lax.rem((hop + (hop % 2) * turn) // 2, 4)
+
+    def copy3(x_first, g, hop):
+        return remote(
+            midway.at[g, hop], moved.at[g, slot3(x_first, hop)],
+            send3.at[g, hop], recv3.at[g, slot3(x_first, hop)],
+            along_z(hop) if x_first else along_x(hop % 2),
+        )
+
+    def far3(x_first, hop):
+        if x_first:
+            return relay if hop else False
+        return relay if hop % 2 else relay & far
+
+    def near3(x_first, hop):
+        if x_first:
+            return False if hop else relay
+        return False if hop % 2 else alone
+
+    def got2(g, hop):
+        return remote(
+            spread.at[g, 0], midway.at[g, hop], send2.at[g, 0], recv2.at[g, hop], along_y(1)
+        )
+
+    def got3(g, slot):
+        return remote(
+            midway.at[g, 0], moved.at[g, slot], send3.at[g, 0], recv3.at[g, slot], along_y(1)
+        )
+
+    def copy4(g, step):
         held = lax.rem(zy - y - step + 8, 4)
         return remote(
             moved.at[g, held], landed.at[g, step],
-            send3.at[g, step], recv3.at[g, step], beside(step),
+            send4.at[g, step], recv4.at[g, step], along_y(step),
         )
 
     def embed(g):
@@ -92,6 +150,54 @@
             hidden = layer(hidden, w_ref[index])
         first[here, :] = hidden
 
+    def second_leg(x_first, g):
+        for step in range(1, 4):
+            copy1(g, step).wait_recv()
+        for m in range(4):
+            if far2(x_first, m) is not False:
+                when(far2(x_first, m), lambda: copy2(x_first, g, m).start())
+            if near2(x_first, m) is not False:
+
+                def keep():
+                    midway[g, hop2(m)] = spread[g, held2(m)]
+
+                when(near2(x_first, m), keep)
+
+    def third_leg(x_first, g):
+        def arrive():
+            for hop in range(8):
+                if x_first:
+                    when(True if hop % 2 else far, lambda: got2(g, hop).wait_recv())
+                elif hop:
+                    got2(g, hop).wait_recv()
+
+        when(relay, arrive)
+        for hop in (4, 3, 5, 2, 6, 1, 7, 0):
+            if far3(x_first, hop) is not False:
+                when(far3(x_first, hop), lambda: copy3(x_first, g, hop).start())
+            if near3(x_first, hop) is not False:
+
+                def keep():
+                    moved[g, slot3(x_first, hop)] = midway[g, hop]
+
+                when(near3(x_first, hop), keep)
+
+    def fourth_leg(x_first, g):
+        for slot in range(4):
+            if x_first:
+                when(True if slot else leaf, lambda: got3(g, slot).wait_recv())
+            else:
+                when(far, lambda: got3(g, slot).wait_recv())
+
+    def by_kind(work, g):
+        @pl.when(lax.rem(g, 2) == 0)
+        def _():
+            work(False, g)
+
+        @pl.when(lax.rem(g, 2) == 1)
+        def _():
+            work(True, g)
+
     def stage(i, carry):
         @pl.when(i < CHUNKS)
         def _():
@@ -106,47 +212,29 @@
 
         @pl.when((i >= 1) & (i <= CHUNKS))
         def _():
-            g = i - 1
+            by_kind(second_leg, i - 1)
+
+        @pl.when((i >= 1 + LAG) & (i <= CHUNKS + LAG))
+        def _():
+            by_kind(third_leg, i - 1 - LAG)
+
+        @pl.when(i == 1 + LAG)
+        def _():
+            total[...] = jnp.zeros_like(total)
+
+        @pl.when((i >= 1 + 2 * LAG) & (i <= CHUNKS + 2 * LAG))
+        def _():
+            g = i - 1 - 2 * LAG
+            by_kind(fourth_leg, g)
             for step in range(1, 4):
-                copy1(g, step).wait_recv()
+                copy4(g, step).start()
+            landed[g, 0] = moved[g, lax.rem(zy - y + 4, 4)]
+
+        @pl.when(i >= 2 + 2 * LAG)
+        def _():
+            g = i - 2 - 2 * LAG
             for step in range(1, 4):
-                copy2(g, step).start()
-
-            @pl.when(alone)
-            def _():
-                stay2(g).start()
-
-            @pl.when(jnp.logical_not(alone))
-            def _():
-                copy2(g, 0).start()
-
-        @pl.when((i >= 1 + LAG) & (i <= CHUNKS + LAG))
-        def _():
-            g = i - 1 - LAG
-            for step in range(1, 4):
-                copy2(g, step).wait_recv()
-
-            @pl.when(alone)
-            def _():
-                stay2(g).wait()
-
-            @pl.when(jnp.logical_not(alone))
-            def _():
-                copy2(g, 0).wait_recv()
-
-            for step in range(1, 4):
-                copy3(g, step).start()
-            landed[g, 0] = moved[g, lax.rem(zy - y + 4, 4)]
-
-        @pl.when(i == 1 + LAG)
-        def _():
-            total[...] = jnp.zeros_like(total)
-
-        @pl.when(i >= 2 + LAG)
-        def _():
-            g = i - 2 - LAG
-            for step in range(1, 4):
-                copy3(g, step).wait_recv()
+                copy4(g, step).wait_recv()
             block = landed[g].reshape(chunk, width)
             lane = lax.broadcasted_iota(jnp.int32, (1, chunk), 1)
             slot, offset = lane // piece, lane % piece
@@ -171,9 +259,15 @@
         return carry
 
     lax.fori_loop(0, rows // 128, widen, 0)
-
-    pl.semaphore_wait(barrier, jnp.where(alone, 6, 7))
-    lax.fori_loop(0, CHUNKS + LAG + 2, stage, 0)
+    pl.semaphore_wait(barrier, jnp.where(settled, 11, 12))
+    lax.fori_loop(0, CHUNKS + 2 * LAG + 2, stage, 0)
+
+    def sent(x_first, g):
+        for m in range(4):
+            when(far2(x_first, m), lambda: copy2(x_first, g, m).wait_send())
+        for hop in range(8):
+            if far3(x_first, hop) is not False:
+                when(far3(x_first, hop), lambda: copy3(x_first, g, hop).wait_send())
 
     def finish(g, carry):
         here = pl.ds(pl.multiple_of(g * chunk, chunk), chunk)
@@ -181,13 +275,8 @@
         joined_ref[here, :] = (both * HALF_ROOT).astype(BF16)
         for step in range(1, 4):
             copy1(g, step).wait_send()
-            copy2(g, step).wait_send()
-            copy3(g, step).wait_send()
-
-        @pl.when(jnp.logical_not(alone))
-        def _():
-            copy2(g, 0).wait_send()
-
+            copy4(g, step).wait_send()
+        by_kind(sent, g)
         return carry
 
     lax.fori_loop(0, CHUNKS, finish, 0)
@@ -196,8 +285,8 @@
 def mirror(edge, w_pre, rev):
     rows, width = edge.shape
     piece = rows // CHUNKS // 4
-    pieces = pltpu.VMEM((CHUNKS, 4, piece, width), BF16)
-    sems = pltpu.SemaphoreType.DMA((CHUNKS, 4))
+    pieces = lambda n: pltpu.VMEM((CHUNKS, n, piece, width), BF16)
+    sems = lambda n: pltpu.SemaphoreType.DMA((CHUNKS, n))
     vmem = pl.BlockSpec(memory_space=pltpu.VMEM)
     return pl.pallas_call(
         mirror_kernel,
@@ -207,10 +296,10 @@
         out_specs=vmem,
         scratch_shapes=[
             pltpu.VMEM((rows, width), BF16),
-            pieces, pieces, pieces,
+            pieces(4), pieces(8), pieces(4), pieces(4),
             pltpu.VMEM((rows, width), F32),
             pltpu.VMEM((rows, 128), jnp.int32),
-            sems, sems, sems, sems, sems, sems,
+            sems(4), sems(4), sems(4), sems(8), sems(8), sems(4), sems(4), sems(4),
         ],
         compiler_params=pltpu.CompilerParams(
             collective_id=0, has_side_effects=True, vmem_limit_bytes=40 << 20

time: 131 us -> 122 us (0.931); the launches traced: 131 us -> 120 us
  Pallas kernels: 125 us -> 115 us
    pallas_call x1, Pallas kernels: 53.1 us -> 22.7 us  [reduce_to_owner(): pl.pallas_call(reduce_kernel, name='reduce_to_owner', out_shape=jax.Shape...]
    pallas_call x1, Pallas kernels: 66.7 us -> 86.8 us  [mirror(): pl.pallas_call(mirror_kernel, name='mirror', out_shape=jax.ShapeDtypeStru...]
where the time goes in v2:
time: 122 us; the launch traced here: 120 us
  Pallas kernels  115 us (94%)
  local copies, waits for them, and re-layouts  4.37 us (4%)
    pallas_call x1, Pallas kernels, mirror(): pl.pallas_call(mirror_kernel, name='mirror', out_shape=jax.ShapeDtypeStru...  86.8 us
    pallas_call x1, Pallas kernels, reduce_to_owner(): pl.pallas_call(reduce_kernel, name='reduce_to_owner', out_shape=jax.Shape...  22.7 us
    pallas_call x1, Pallas kernels, messages(): pl.pallas_call(message_kernel, name='messages', grid=(rows // tile,), out...  5.59 us
    unnamed x15, local copies, waits for them, and re-layouts  4.37 us

profile of v2, /device:TPU:1, one launch (start us, length us, event | category | flops | bytes accessed | tf_op | source)
XLA Modules:
  0.0 120.2 jit_solution(3807362165025968214)
XLA Ops:
  0.0 0.0 copy-start
  0.0 1.6 %copy-done = bf16[1,1,2048,512]{3,2,1,0:T(8,128)(2,1)S(1)} copy-done((bf16[1,1,2048,512]{3,2,1,0:T(8,128)(2,1)S(1)}, bf16[1,1,2048,512]{3,2,1,0:T(8,128)(2,1)}, u32[]{:S(2)}) %copy-start) | copy-done | bytes 2097176
  1.6 0.0 copy-start.2
  1.6 1.4 %copy-done.2 = bf16[3,512,512]{2,1,0:T(8,128)(2,1)S(1)} copy-done((bf16[3,512,512]{2,1,0:T(8,128)(2,1)S(1)}, bf16[3,512,512]{2,1,0:T(8,128)(2,1)}, u32[]{:S(2)}) %copy-start.2) | copy-done | bytes 1572888
  3.0 0.0 copy-start.4
  3.0 0.7 copy-done.4
  3.7 0.0 copy-start.1
  3.7 0.0 copy-start.3
  3.7 86.8 %mirror.1.joined_ref = bf16[2048,512]{1,0:T(8,128)(2,1)S(1)} custom-call(bf16[2048,512]{1,0:T(8,128)(2,1)S(1)} %bitcast.4, bf16[3,512,512]{2,1,0:T(8,128)(2,1)S(1)} %copy-done.2, s32[1,2048]{1,0:T(1,128)S(1)} %bitcast.6), custom_call_target="tpu_custom_call" | custom-call | tf_op jit(solution)/shard_map/mirror/pallas_call | solution.py:291
  90.5 0.0 copy-done.1
  90.5 0.0 copy-done.3
  90.5 0.0 copy-start.5
  90.5 0.0 copy-start.6
  90.5 5.6 %messages.1.message_ref = bf16[2048,256]{1,0:T(8,128)(2,1)S(1)} custom-call(bf16[2048,512]{1,0:T(8,128)(2,1)S(1)} %mirror.1.joined_ref, bf16[3,512,512]{2,1,0:T(8,128)(2,1)S(1)} %copy-done.1, bf16[512,256]{1,0:T(8,128)(2,1)S(1)} %copy-done.3), custom_call_target="tpu_custom_call" | custom-call | tf_op jit(solution)/shard_map/messages/pallas_call | solution.py:320
  96.8 0.0 copy-done.5
  96.8 0.0 copy-done.6
  96.8 22.7 %reduce_to_owner.1 = bf16[256,256]{1,0:T(8,128)(2,1)S(1)} custom-call(bf16[2048,256]{1,0:T(8,128)(2,1)S(1)} %messages.1.message_ref, s32[1,2048]{1,0:T(1,128)S(1)} %bitcast.7, s32[1,1]{1,0:T(1,128)S(6)} %copy.10.count_ref, s32[1,16]{1,0:T(1,128)S(1)} %copy-done.6), custom_call_target="tpu_custom_call" | custom-call | tf_op jit(solution)/shard_map/reduce_to_owner/pallas_call | solution.py:421
  119.5 0.7 copy.11
Async XLA Ops:
  0.0 1.6 %copy-start = (bf16[1,1,2048,512]{3,2,1,0:T(8,128)(2,1)S(1)}, bf16[1,1,2048,512]{3,2,1,0:T(8,128)(2,1)}, u32[]{:S(2)}) copy-start(bf16[1,1,2048,512]{3,2,1,0:T(8,128)(2,1)} %param.8) | copy-start | bytes 6291460
  1.6 1.4 %copy-start.2 = (bf16[3,512,512]{2,1,0:T(8,128)(2,1)S(1)}, bf16[3,512,512]{2,1,0:T(8,128)(2,1)}, u32[]{:S(2)}) copy-start(bf16[3,512,512]{2,1,0:T(8,128)(2,1)} %w_ref.2) | copy-start | bytes 4718596
  3.0 0.7 copy-start.4
  3.7 86.8 %copy-start.1 = (bf16[3,512,512]{2,1,0:T(8,128)(2,1)S(1)}, bf16[3,512,512]{2,1,0:T(8,128)(2,1)}, u32[]{:S(2)}) copy-start(bf16[3,512,512]{2,1,0:T(8,128)(2,1)} %w_ref.3) | copy-start | bytes 4718596
  3.7 86.8 %copy-start.3 = (bf16[512,256]{1,0:T(8,128)(2,1)S(1)}, bf16[512,256]{1,0:T(8,128)(2,1)}, u32[]{:S(2)}) copy-start(bf16[512,256]{1,0:T(8,128)(2,1)} %w_out_ref.1) | copy-start | bytes 786436
  90.5 6.3 %copy-start.5 = (s32[1,1,2048]{2,1,0:T(1,128)S(1)}, s32[1,1,2048]{2,1,0:T(1,128)}, u32[]{:S(2)}) copy-start(s32[1,1,2048]{2,1,0:T(1,128)} %param.11) | copy-start | bytes 24580
  90.5 6.3 %copy-start.6 = (s32[1,16]{1,0:T(1,128)S(1)}, s32[1,16]{1,0:T(1,128)}, u32[]{:S(2)}) copy-start(s32[1,16]{1,0:T(1,128)} %owner_ref.1) | copy-start | bytes 196

commit v3 on v2

--- a/solution.py
+++ b/solution.py
@@ -12,7 +12,7 @@
 SRC = ("y", "xh", "c")
 TGT = ("z", "xl")
 CHUNKS = 8
-LAG = 2
+LAGS = (2, 2, 2, 2)
 F32 = jnp.float32
 BF16 = jnp.bfloat16
 
@@ -210,29 +210,28 @@
         def _():
             embed(i + 1)
 
-        @pl.when((i >= 1) & (i <= CHUNKS))
-        def _():
-            by_kind(second_leg, i - 1)
-
-        @pl.when((i >= 1 + LAG) & (i <= CHUNKS + LAG))
-        def _():
-            by_kind(third_leg, i - 1 - LAG)
-
-        @pl.when(i == 1 + LAG)
+        for g, leg in ((i - LAGS[0], second_leg), (i - sum(LAGS[:2]), third_leg)):
+
+            @pl.when((g >= 0) & (g < CHUNKS))
+            def _():
+                by_kind(leg, g)
+
+        @pl.when(i == 2)
         def _():
             total[...] = jnp.zeros_like(total)
 
-        @pl.when((i >= 1 + 2 * LAG) & (i <= CHUNKS + 2 * LAG))
-        def _():
-            g = i - 1 - 2 * LAG
+        g = i - sum(LAGS[:3])
+
+        @pl.when((g >= 0) & (g < CHUNKS))
+        def _():
             by_kind(fourth_leg, g)
             for step in range(1, 4):
                 copy4(g, step).start()
             landed[g, 0] = moved[g, lax.rem(zy - y + 4, 4)]
 
-        @pl.when(i >= 2 + 2 * LAG)
-        def _():
-            g = i - 2 - 2 * LAG
+        @pl.when(i >= sum(LAGS))
+        def _():
+            g = i - sum(LAGS)
             for step in range(1, 4):
                 copy4(g, step).wait_recv()
             block = landed[g].reshape(chunk, width)
@@ -260,7 +259,7 @@
 
     lax.fori_loop(0, rows // 128, widen, 0)
     pl.semaphore_wait(barrier, jnp.where(settled, 11, 12))
-    lax.fori_loop(0, CHUNKS + 2 * LAG + 2, stage, 0)
+    lax.fori_loop(0, CHUNKS + sum(LAGS), stage, 0)
 
     def sent(x_first, g):
         for m in range(4):
@@ -307,139 +306,178 @@
     )(edge, w_pre, rev)
 
 
-def message_kernel(joined_ref, w_ref, w_out_ref, message_ref):
-    hidden = joined_ref[...]
-    for index in range(w_ref.shape[0]):
-        hidden = layer(hidden, w_ref[index])
-    message_ref[...] = jnp.dot(hidden, w_out_ref[...], preferred_element_type=F32).astype(BF16)
-
-
-def messages(joined, w_post, w_out):
-    rows, width = joined.shape
-    tile = 512
-    return pl.pallas_call(
-        message_kernel,
-        name="messages",
-        grid=(rows // tile,),
-        out_shape=jax.ShapeDtypeStruct((rows, w_out.shape[1]), BF16),
-        in_specs=[
-            pl.BlockSpec((tile, width), lambda i: (i, 0)),
-            pl.BlockSpec(w_post.shape, lambda i: (0, 0, 0)),
-            pl.BlockSpec(w_out.shape, lambda i: (0, 0)),
-        ],
-        out_specs=pl.BlockSpec((tile, w_out.shape[1]), lambda i: (i, 0)),
-        compiler_params=pltpu.CompilerParams(vmem_limit_bytes=24 << 20),
-    )(joined, w_post, w_out)
-
-
-HOPS = ((2, 1), (1, 1), (3, 1), (2, 0), (0, 1), (1, 0), (3, 0), (0, 0))
-
-
-def reduce_kernel(
-    message_ref, atom_ref, count_ref, owner_ref, out_ref,
-    target, mine, pair_out, pair_in, far_out, far_in,
-    pair_send, pair_recv, far_send, far_recv,
+HOPS = ((2, 1), (1, 1), (3, 1), (0, 1), (2, 0), (1, 0), (3, 0), (0, 0))
+
+
+def owner_kernel(
+    joined_ref, w_ref, w_out_ref, atom_ref, count_ref, owner_ref, out_ref,
+    message, match, place, pair_out, pair_in, mine,
+    left_y_out, left_y_in, left_x_out, left_x_in, left_keep,
+    right_x_out, right_x_in, right_y_out, right_y_in, right_keep,
+    pair_send, pair_recv, left_y_send, left_y_recv, left_x_send, left_x_recv,
+    right_x_send, right_x_recv, right_y_send, right_y_recv,
 ):
     y, xh, c, z, xl = where_am_i()
-    edges, width = message_ref.shape
+    edges, width = message.shape
+    half = width // 2
     other = (y, xh, 1 - c, z, xl)
-
-    def owner_of(hop):
-        return lax.rem(y + HOPS[hop][0], 4), lax.rem(xh + HOPS[hop][1], 2)
-
-    def far_device(hop):
-        return (*owner_of(hop), c, z, xl)
+    across = (y, 1 - xh, c, z, xl)
+
+    def along_y(step):
+        return (lax.rem(y + step, 4), xh, c, z, xl)
 
     barrier = pltpu.get_barrier_semaphore()
-    pl.semaphore_signal(barrier, inc=1, device_id=other, device_id_type=MESH)
-    for hop in range(7):
-        pl.semaphore_signal(barrier, inc=1, device_id=far_device(hop), device_id_type=MESH)
+    for device in (other, across, along_y(1), along_y(2), along_y(3)):
+        pl.semaphore_signal(barrier, inc=1, device_id=device, device_id_type=MESH)
 
     atoms = atom_ref[...]
-    block = atoms // SUB
-    place = jnp.zeros_like(atoms)
+    owner = jnp.zeros_like(atoms)
     for k in range(owner_ref.shape[1]):
-        place = jnp.where(block == k, owner_ref[0, k], place)
-    slot = lax.broadcasted_iota(jnp.int32, atoms.shape, 1)
-    target[...] = jnp.where(slot < count_ref[0, 0], place * SUB + atoms % SUB, -1)
-    pl.semaphore_wait(barrier, 8)
-
+        owner = jnp.where(atoms // SUB == k, owner_ref[0, k], owner)
+    edge = lax.broadcasted_iota(jnp.int32, atoms.shape, 1)
+    place[...] = jnp.where(edge < count_ref[0, 0], owner, -1)
     row = lax.broadcasted_iota(jnp.int32, (SUB, edges), 0)
-
-    def part(position):
-        select = jnp.where(row == target[...] - position * SUB, 1.0, 0.0).astype(BF16)
-        return jnp.dot(select, message_ref[...], preferred_element_type=F32)
+    match[...] = jnp.where(row == atoms % SUB, 1.0, 0.0).astype(BF16)
+
+    def tell(t, carry):
+        some = pl.ds(pl.multiple_of(t * 512, 512), 512)
+        hidden = joined_ref[some, :]
+        for index in range(w_ref.shape[0]):
+            hidden = layer(hidden, w_ref[index])
+        message[some, :] = jnp.dot(
+            hidden, w_out_ref[...], preferred_element_type=F32
+        ).astype(BF16)
+        return carry
+
+    lax.fori_loop(0, edges // 512, tell, 0)
+    pl.semaphore_wait(barrier, 5)
+
+    def copy(out, into, send, recv, index, device):
+        return pltpu.make_async_remote_copy(
+            src_ref=out.at[index], dst_ref=into.at[index],
+            send_sem=send.at[index], recv_sem=recv.at[index],
+            device_id=device, device_id_type=MESH,
+        )
 
     def pair_copy(hop):
-        return pltpu.make_async_remote_copy(
-            src_ref=pair_out.at[hop], dst_ref=pair_in.at[hop],
-            send_sem=pair_send.at[hop], recv_sem=pair_recv.at[hop],
-            device_id=other, device_id_type=MESH,
-        )
-
-    def far_copy(hop):
-        return pltpu.make_async_remote_copy(
-            src_ref=far_out.at[hop], dst_ref=far_in.at[hop],
-            send_sem=far_send.at[hop], recv_sem=far_recv.at[hop],
-            device_id=far_device(hop), device_id_type=MESH,
-        )
-
-    def send_on(hop):
+        return copy(pair_out, pair_in, pair_send, pair_recv, hop, other)
+
+    def left_y(dy, dx):
+        return copy(
+            left_y_out, left_y_in, left_y_send, left_y_recv, 2 * (dy - 1) + dx, along_y(dy)
+        )
+
+    def left_x():
+        return copy(left_x_out, left_x_in, left_x_send, left_x_recv, 0, across)
+
+    def right_x(dy):
+        return copy(right_x_out, right_x_in, right_x_send, right_x_recv, dy, across)
+
+    def right_y(dy):
+        return copy(right_y_out, right_y_in, right_y_send, right_y_recv, dy - 1, along_y(dy))
+
+    def compute(hop):
+        dy, dx = HOPS[hop]
+        position = 4 * lax.rem(y + dy, 4) + 2 * lax.rem(xh + dx, 2)
+
+        def chosen(at):
+            return match[...] * jnp.where(place[...] == at, 1.0, 0.0).astype(BF16)
+
+        select = jnp.concatenate([chosen(position + 1 - c), chosen(position + c)], axis=0)
+        sums = jnp.dot(select, message[...], preferred_element_type=F32)
+        pair_out[hop] = sums[:SUB].astype(BF16)
+        pair_copy(hop).start()
+        mine[hop % 2] = sums[SUB:]
+
+    def pass_on(hop):
+        dy, dx = HOPS[hop]
         pair_copy(hop).wait_recv()
         chip_sum = mine[hop % 2] + pair_in[hop].astype(F32)
-        if hop < 7:
-            far_out[hop] = chip_sum.astype(BF16)
-            far_copy(hop).start()
-            return None
-        return chip_sum
-
-    for hop in range(8):
-        to_y, to_xh = owner_of(hop)
-        position = 4 * to_y + 2 * to_xh
-        pair_out[hop] = part(position + 1 - c).astype(BF16)
-        pair_copy(hop).start()
-        mine[hop % 2] = part(position + c)
-        if hop > 0:
-            send_on(hop - 1)
-    result = send_on(7)
-    for hop in range(7):
-        far_copy(hop).wait_recv()
-        result = result + far_in[hop].astype(F32)
-    out_ref[...] = result.astype(BF16)
+        if dy:
+            left_y_out[2 * (dy - 1) + dx] = chip_sum[:, :half].astype(BF16)
+            left_y(dy, dx).start()
+        else:
+            left_keep[dx] = chip_sum[:, :half]
+        if dx:
+            right_x_out[dy] = chip_sum[:, half:].astype(BF16)
+            right_x(dy).start()
+        else:
+            right_keep[dy] = chip_sum[:, half:]
+
+    compute(0)
+    for hop in range(1, 8):
+        compute(hop)
+        pass_on(hop - 1)
+    pass_on(7)
+
+    for dy in (2, 1, 3):
+        right_x(dy).wait_recv()
+        right_y_out[dy - 1] = (right_keep[dy] + right_x_in[dy].astype(F32)).astype(BF16)
+        right_y(dy).start()
+
+    def gathered(dx):
+        value = left_keep[dx]
+        for dy in (2, 1, 3):
+            left_y(dy, dx).wait_recv()
+            value = value + left_y_in[2 * (dy - 1) + dx].astype(F32)
+        return value
+
+    left_x_out[0] = gathered(1).astype(BF16)
+    left_x().start()
+    left_sum = gathered(0)
+    right_x(0).wait_recv()
+    right_sum = right_keep[0] + right_x_in[0].astype(F32)
+    for dy in (1, 3, 2):
+        right_y(dy).wait_recv()
+        right_sum = right_sum + right_y_in[dy - 1].astype(F32)
+    out_ref[:, half:] = right_sum.astype(BF16)
+    left_x().wait_recv()
+    out_ref[:, :half] = (left_sum + left_x_in[0].astype(F32)).astype(BF16)
+
     for hop in range(8):
         pair_copy(hop).wait_send()
-    for hop in range(7):
-        far_copy(hop).wait_send()
-
-
-def reduce_to_owner(message, atoms, count, owners):
-    width = message.shape[1]
-    blocks = lambda n: pltpu.VMEM((n, SUB, width), BF16)
-    sems = pltpu.SemaphoreType.DMA((8,))
+    left_x().wait_send()
+    for dy in range(4):
+        right_x(dy).wait_send()
+    for dy in (1, 2, 3):
+        right_y(dy).wait_send()
+        for dx in (0, 1):
+            left_y(dy, dx).wait_send()
+
+
+def owner_sums(joined, w_post, w_out, atoms, count, owners):
+    edges, width = joined.shape[0], w_out.shape[1]
+    whole = lambda n, kind=BF16: pltpu.VMEM((n, SUB, width), kind)
+    halves = lambda n, kind=BF16: pltpu.VMEM((n, SUB, width // 2), kind)
+    sems = lambda n: pltpu.SemaphoreType.DMA((n,))
     vmem = pl.BlockSpec(memory_space=pltpu.VMEM)
     smem = pl.BlockSpec(memory_space=pltpu.SMEM)
     return pl.pallas_call(
-        reduce_kernel,
-        name="reduce_to_owner",
+        owner_kernel,
+        name="owner_sums",
         out_shape=jax.ShapeDtypeStruct((SUB, width), BF16),
-        in_specs=[vmem, vmem, smem, smem],
+        in_specs=[vmem, vmem, vmem, vmem, smem, smem],
         out_specs=vmem,
         scratch_shapes=[
+            pltpu.VMEM((edges, width), BF16),
+            pltpu.VMEM((SUB, edges), BF16),
             pltpu.VMEM(atoms.shape, jnp.int32),
-            pltpu.VMEM((2, SUB, width), F32),
-            blocks(8), blocks(8), blocks(7), blocks(7),
-            sems, sems, sems, sems,
+            whole(8), whole(8), whole(2, F32),
+            halves(6), halves(6), halves(1), halves(1), halves(2, F32),
+            halves(4), halves(4), halves(3), halves(3), halves(4, F32),
+            sems(8), sems(8), sems(6), sems(6), sems(1), sems(1),
+            sems(4), sems(4), sems(3), sems(3),
         ],
         compiler_params=pltpu.CompilerParams(
-            collective_id=1, has_side_effects=True, vmem_limit_bytes=24 << 20
+            collective_id=1, has_side_effects=True, vmem_limit_bytes=32 << 20
         ),
-    )(message, atoms, count, owners)
+    )(joined, w_post, w_out, atoms, count, owners)
 
 
 def shards(edge_feat, tile_counts, reverse_rows, incidence, owner_map, w_pre, w_post, w_out):
     joined = mirror(edge_feat[0, 0], w_pre, reverse_rows[0])
-    message = messages(joined, w_post, w_out)
-    return reduce_to_owner(message, incidence[0], tile_counts, owner_map)[None]
+    sums = owner_sums(joined, w_post, w_out, incidence[0], tile_counts, owner_map)
+    return sums[None]
 
 
 def solution(mesh):

time: 122 us -> 117 us (0.959); the launches traced: 120 us -> 117 us
  Pallas kernels: 115 us -> 112 us
    pallas_call x2 -> x1, Pallas kernels: 28.3 us -> 23.8 us  [owner_sums(): pl.pallas_call(owner_kernel, name='owner_sums', out_shape=jax.ShapeDtypeS...]
where the time goes in v3:
time: 117 us
  Pallas kernels  112 us (96%)
  local copies, waits for them, and re-layouts  4.36 us (4%)
    pallas_call x1, Pallas kernels, mirror(): pl.pallas_call(mirror_kernel, name='mirror', out_shape=jax.ShapeDtypeStru...  87.9 us
    pallas_call x1, Pallas kernels, owner_sums(): pl.pallas_call(owner_kernel, name='owner_sums', out_shape=jax.ShapeDtypeS...  23.8 us
    unnamed x15, local copies, waits for them, and re-layouts  4.36 us

profile of v3, /device:TPU:1, one launch (start us, length us, event | category | flops | bytes accessed | tf_op | source)
XLA Modules:
  0.0 116.7 jit_solution(14944955714981575678)
XLA Ops:
  0.7 0.0 copy-start
  0.7 1.6 %copy-done = bf16[1,1,2048,512]{3,2,1,0:T(8,128)(2,1)S(1)} copy-done((bf16[1,1,2048,512]{3,2,1,0:T(8,128)(2,1)S(1)}, bf16[1,1,2048,512]{3,2,1,0:T(8,128)(2,1)}, u32[]{:S(2)}) %copy-start) | copy-done | bytes 2097176
  2.2 0.0 copy-start.2
  2.2 1.4 %copy-done.2 = bf16[3,512,512]{2,1,0:T(8,128)(2,1)S(1)} copy-done((bf16[3,512,512]{2,1,0:T(8,128)(2,1)S(1)}, bf16[3,512,512]{2,1,0:T(8,128)(2,1)}, u32[]{:S(2)}) %copy-start.2) | copy-done | bytes 1572888
  3.7 0.0 copy-start.4
  3.7 0.7 copy-done.4
  4.4 0.0 copy-start.1
  4.4 0.0 copy-start.3
  4.4 0.0 copy-start.5
  4.4 0.0 copy-start.6
  4.4 87.9 %mirror.1.joined_ref = bf16[2048,512]{1,0:T(8,128)(2,1)S(1)} custom-call(bf16[2048,512]{1,0:T(8,128)(2,1)S(1)} %bitcast.4, bf16[3,512,512]{2,1,0:T(8,128)(2,1)S(1)} %copy-done.2, s32[1,2048]{1,0:T(1,128)S(1)} %bitcast.6), custom_call_target="tpu_custom_call" | custom-call | tf_op jit(solution)/shard_map/mirror/pallas_call | solution.py:290
  92.3 0.0 copy-done.1
  92.3 0.0 copy-done.3
  92.3 0.0 copy-done.5
  92.3 0.0 copy-done.6
  92.3 23.8 %owner_sums.1 = bf16[256,256]{1,0:T(8,128)(2,1)S(1)} custom-call(bf16[2048,512]{1,0:T(8,128)(2,1)S(1)} %mirror.1.joined_ref, bf16[3,512,512]{2,1,0:T(8,128)(2,1)S(1)} %copy-done.1, bf16[512,256]{1,0:T(8,128)(2,1)S(1)} %copy-done.3, s32[1,2048]{1,0:T(1,128)S(1)} %bitcast.7, s32[1,1]{1,0:T(1,128)S(6)} %copy.10.count_ref, s32[1,16]{1,0:T(1,128)S(1)} %copy-done.6), custom_call_target="tpu_custom_call" | custom-call | tf_op jit(solution)/shard_map/owner_sums/pallas_call | solution.py:455
  116.1 0.7 copy.11
Async XLA Ops:
  0.7 1.6 %copy-start = (bf16[1,1,2048,512]{3,2,1,0:T(8,128)(2,1)S(1)}, bf16[1,1,2048,512]{3,2,1,0:T(8,128)(2,1)}, u32[]{:S(2)}) copy-start(bf16[1,1,2048,512]{3,2,1,0:T(8,128)(2,1)} %param.8) | copy-start | bytes 6291460
  2.2 1.4 %copy-start.2 = (bf16[3,512,512]{2,1,0:T(8,128)(2,1)S(1)}, bf16[3,512,512]{2,1,0:T(8,128)(2,1)}, u32[]{:S(2)}) copy-start(bf16[3,512,512]{2,1,0:T(8,128)(2,1)} %w_ref.2) | copy-start | bytes 4718596
  3.7 0.7 copy-start.4
  4.4 87.9 %copy-start.1 = (bf16[3,512,512]{2,1,0:T(8,128)(2,1)S(1)}, bf16[3,512,512]{2,1,0:T(8,128)(2,1)}, u32[]{:S(2)}) copy-start(bf16[3,512,512]{2,1,0:T(8,128)(2,1)} %w_ref.3) | copy-start | bytes 4718596
  4.4 87.9 %copy-start.3 = (bf16[512,256]{1,0:T(8,128)(2,1)S(1)}, bf16[512,256]{1,0:T(8,128)(2,1)}, u32[]{:S(2)}) copy-start(bf16[512,256]{1,0:T(8,128)(2,1)} %w_out_ref.1) | copy-start | bytes 786436
  4.4 87.9 %copy-start.5 = (s32[1,1,2048]{2,1,0:T(1,128)S(1)}, s32[1,1,2048]{2,1,0:T(1,128)}, u32[]{:S(2)}) copy-start(s32[1,1,2048]{2,1,0:T(1,128)} %param.11) | copy-start | bytes 24580
  4.4 87.9 %copy-start.6 = (s32[1,16]{1,0:T(1,128)S(1)}, s32[1,16]{1,0:T(1,128)}, u32[]{:S(2)}) copy-start(s32[1,16]{1,0:T(1,128)} %owner_ref.1) | copy-start | bytes 196

commit v4 on v3

--- a/solution.py
+++ b/solution.py
@@ -12,7 +12,7 @@
 SRC = ("y", "xh", "c")
 TGT = ("z", "xl")
 CHUNKS = 8
-LAGS = (2, 2, 2, 2)
+LAGS = (2, 3, 3, 2)
 F32 = jnp.float32
 BF16 = jnp.bfloat16
 
@@ -29,8 +29,8 @@
 
 def mirror_kernel(
     edge_ref, w_ref, rev_ref, joined_ref,
-    first, spread, midway, moved, landed, total, rev_wide,
-    send1, recv1, send2, recv2, send3, recv3, send4, recv4,
+    first, spread, midway, moved, landed, detour, total, rev_wide,
+    send1, recv1, send2, recv2, send3, recv3, send4, recv4, recv5, send6,
 ):
     y, xh, c, z, xl = where_am_i()
     zy, z0 = z // 2, lax.rem(z, 2)
@@ -100,7 +100,7 @@
         )
 
     def far2(x_first, m):
-        return far if x_first else (leaf if m == 0 else True)
+        return far if x_first else (leaf if m in (0, 2) else True)
 
     def near2(x_first, m):
         return alone if x_first else (relay if m == 0 else False)
@@ -118,7 +118,7 @@
 
     def far3(x_first, hop):
         if x_first:
-            return relay if hop else False
+            return relay if hop % 4 else False
         return relay if hop % 2 else relay & far
 
     def near3(x_first, hop):
@@ -135,6 +135,24 @@
         return remote(
             midway.at[g, 0], moved.at[g, slot], send3.at[g, 0], recv3.at[g, slot], along_y(1)
         )
+
+    def detour_out(x_first, g):
+        return remote(
+            midway.at[g, 4] if x_first else spread.at[g, held2(2)], detour.at[g],
+            send3.at[g, 4] if x_first else send2.at[g, 2], recv5.at[g], along_z(2 + 4 * c),
+        )
+
+    def detour_on(x_first, g):
+        return remote(
+            detour.at[g], moved.at[g, 2] if x_first else midway.at[g, 4],
+            send6.at[g], recv3.at[g, 2] if x_first else recv2.at[g, 4], along_z(2 + 4 * c),
+        )
+
+    def detour_leg(x_first, g):
+        @pl.when(relay)
+        def _():
+            detour_out(x_first, g).wait_recv()
+            detour_on(x_first, g).start()
 
     def copy4(g, step):
         held = lax.rem(zy - y - step + 8, 4)
@@ -162,6 +180,8 @@
                     midway[g, hop2(m)] = spread[g, held2(m)]
 
                 when(near2(x_first, m), keep)
+            if m == 2 and not x_first:
+                when(relay, lambda: detour_out(False, g).start())
 
     def third_leg(x_first, g):
         def arrive():
@@ -181,6 +201,8 @@
                     moved[g, slot3(x_first, hop)] = midway[g, hop]
 
                 when(near3(x_first, hop), keep)
+            if hop == 4 and x_first:
+                when(relay, lambda: detour_out(True, g).start())
 
     def fourth_leg(x_first, g):
         for slot in range(4):
@@ -210,11 +232,17 @@
         def _():
             embed(i + 1)
 
-        for g, leg in ((i - LAGS[0], second_leg), (i - sum(LAGS[:2]), third_leg)):
-
-            @pl.when((g >= 0) & (g < CHUNKS))
-            def _():
-                by_kind(leg, g)
+        def run(g, leg, kinds=(False, True)):
+            for x_first in kinds:
+
+                @pl.when((g >= 0) & (g < CHUNKS) & (lax.rem(g + 2, 2) == int(x_first)))
+                def _():
+                    leg(x_first, g)
+
+        run(i - LAGS[0], second_leg)
+        run(i - LAGS[0] - 1, detour_leg, (False,))
+        run(i - sum(LAGS[:2]), third_leg)
+        run(i - sum(LAGS[:2]) - 1, detour_leg, (True,))
 
         @pl.when(i == 2)
         def _():
@@ -267,6 +295,12 @@
         for hop in range(8):
             if far3(x_first, hop) is not False:
                 when(far3(x_first, hop), lambda: copy3(x_first, g, hop).wait_send())
+
+        @pl.when(relay)
+        def _():
+            detour_out(x_first, g).wait_send()
+            detour_on(x_first, g).wait_send()
+
 
     def finish(g, carry):
         here = pl.ds(pl.multiple_of(g * chunk, chunk), chunk)
@@ -296,9 +330,11 @@
         scratch_shapes=[
             pltpu.VMEM((rows, width), BF16),
             pieces(4), pieces(8), pieces(4), pieces(4),
+            pltpu.VMEM((CHUNKS, piece, width), BF16),
             pltpu.VMEM((rows, width), F32),
             pltpu.VMEM((rows, 128), jnp.int32),
             sems(4), sems(4), sems(4), sems(8), sems(8), sems(4), sems(4), sems(4),
+            pltpu.SemaphoreType.DMA((CHUNKS,)), pltpu.SemaphoreType.DMA((CHUNKS,)),
         ],
         compiler_params=pltpu.CompilerParams(
             collective_id=0, has_side_effects=True, vmem_limit_bytes=40 << 20

time: 117 us -> 108 us (0.923)
  Pallas kernels: 112 us -> 102 us
    pallas_call x1, Pallas kernels: 87.9 us -> 76.7 us  [mirror(): pl.pallas_call(mirror_kernel, name='mirror', out_shape=jax.ShapeDtypeStru...]
    pallas_call x1, Pallas kernels: 23.8 us -> 25.7 us  [owner_sums(): pl.pallas_call(owner_kernel, name='owner_sums', out_shape=jax.ShapeDtypeS...]
where the time goes in v4:
time: 108 us
  Pallas kernels  102 us (94%)
  local copies, waits for them, and re-layouts  4.36 us (4%)
    pallas_call x1, Pallas kernels, mirror(): pl.pallas_call(mirror_kernel, name='mirror', out_shape=jax.ShapeDtypeStru...  76.7 us
    pallas_call x1, Pallas kernels, owner_sums(): pl.pallas_call(owner_kernel, name='owner_sums', out_shape=jax.ShapeDtypeS...  25.7 us
    unnamed x15, local copies, waits for them, and re-layouts  4.36 us

profile of v4, /device:TPU:1, one launch (start us, length us, event | category | flops | bytes accessed | tf_op | source)
XLA Modules:
  0.0 107.6 jit_solution(6950415799150533523)
XLA Ops:
  0.7 0.0 copy-start
  0.7 1.6 %copy-done = bf16[1,1,2048,512]{3,2,1,0:T(8,128)(2,1)S(1)} copy-done((bf16[1,1,2048,512]{3,2,1,0:T(8,128)(2,1)S(1)}, bf16[1,1,2048,512]{3,2,1,0:T(8,128)(2,1)}, u32[]{:S(2)}) %copy-start) | copy-done | bytes 2097176
  2.2 0.0 copy-start.2
  2.2 1.4 %copy-done.2 = bf16[3,512,512]{2,1,0:T(8,128)(2,1)S(1)} copy-done((bf16[3,512,512]{2,1,0:T(8,128)(2,1)S(1)}, bf16[3,512,512]{2,1,0:T(8,128)(2,1)}, u32[]{:S(2)}) %copy-start.2) | copy-done | bytes 1572888
  3.7 0.0 copy-start.4
  3.7 0.7 copy-done.4
  4.4 0.0 copy-start.1
  4.4 0.0 copy-start.3
  4.4 0.0 copy-start.5
  4.4 0.0 copy-start.6
  4.4 76.7 %mirror.1.joined_ref = bf16[2048,512]{1,0:T(8,128)(2,1)S(1)} custom-call(bf16[2048,512]{1,0:T(8,128)(2,1)S(1)} %bitcast.4, bf16[3,512,512]{2,1,0:T(8,128)(2,1)S(1)} %copy-done.2, s32[1,2048]{1,0:T(1,128)S(1)} %bitcast.6), custom_call_target="tpu_custom_call" | custom-call | tf_op jit(solution)/shard_map/mirror/pallas_call | solution.py:324
  81.1 0.0 copy-done.1
  81.1 0.0 copy-done.3
  81.1 0.0 copy-done.5
  81.1 0.0 copy-done.6
  81.2 25.7 %owner_sums.1 = bf16[256,256]{1,0:T(8,128)(2,1)S(1)} custom-call(bf16[2048,512]{1,0:T(8,128)(2,1)S(1)} %mirror.1.joined_ref, bf16[3,512,512]{2,1,0:T(8,128)(2,1)S(1)} %copy-done.1, bf16[512,256]{1,0:T(8,128)(2,1)S(1)} %copy-done.3, s32[1,2048]{1,0:T(1,128)S(1)} %bitcast.7, s32[1,1]{1,0:T(1,128)S(6)} %copy.10.count_ref, s32[1,16]{1,0:T(1,128)S(1)} %copy-done.6), custom_call_target="tpu_custom_call" | custom-call | tf_op jit(solution)/shard_map/owner_sums/pallas_call | solution.py:491
  106.9 0.7 copy.11
Async XLA Ops:
  0.7 1.6 %copy-start = (bf16[1,1,2048,512]{3,2,1,0:T(8,128)(2,1)S(1)}, bf16[1,1,2048,512]{3,2,1,0:T(8,128)(2,1)}, u32[]{:S(2)}) copy-start(bf16[1,1,2048,512]{3,2,1,0:T(8,128)(2,1)} %param.8) | copy-start | bytes 6291460
  2.2 1.4 %copy-start.2 = (bf16[3,512,512]{2,1,0:T(8,128)(2,1)S(1)}, bf16[3,512,512]{2,1,0:T(8,128)(2,1)}, u32[]{:S(2)}) copy-start(bf16[3,512,512]{2,1,0:T(8,128)(2,1)} %w_ref.2) | copy-start | bytes 4718596
  3.7 0.7 copy-start.4
  4.4 76.8 %copy-start.1 = (bf16[3,512,512]{2,1,0:T(8,128)(2,1)S(1)}, bf16[3,512,512]{2,1,0:T(8,128)(2,1)}, u32[]{:S(2)}) copy-start(bf16[3,512,512]{2,1,0:T(8,128)(2,1)} %w_ref.3) | copy-start | bytes 4718596
  4.4 76.8 %copy-start.3 = (bf16[512,256]{1,0:T(8,128)(2,1)S(1)}, bf16[512,256]{1,0:T(8,128)(2,1)}, u32[]{:S(2)}) copy-start(bf16[512,256]{1,0:T(8,128)(2,1)} %w_out_ref.1) | copy-start | bytes 786436
  4.4 76.8 %copy-start.5 = (s32[1,1,2048]{2,1,0:T(1,128)S(1)}, s32[1,1,2048]{2,1,0:T(1,128)}, u32[]{:S(2)}) copy-start(s32[1,1,2048]{2,1,0:T(1,128)} %param.11) | copy-start | bytes 24580
  4.4 76.8 %copy-start.6 = (s32[1,16]{1,0:T(1,128)S(1)}, s32[1,16]{1,0:T(1,128)}, u32[]{:S(2)}) copy-start(s32[1,16]{1,0:T(1,128)} %owner_ref.1) | copy-start | bytes 196

commit v5 on v4

--- a/solution.py
+++ b/solution.py
@@ -13,6 +13,7 @@
 TGT = ("z", "xl")
 CHUNKS = 8
 LAGS = (2, 3, 3, 2)
+VMEM_BYTES = 62 << 20
 F32 = jnp.float32
 BF16 = jnp.bfloat16
 
@@ -27,10 +28,18 @@
     return tuple(lax.axis_index(name) for name in ("y", "xh", "c", "z", "xl"))
 
 
-def mirror_kernel(
-    edge_ref, w_ref, rev_ref, joined_ref,
-    first, spread, midway, moved, landed, detour, total, rev_wide,
+HOPS = ((2, 1), (1, 1), (3, 1), (0, 1), (2, 0), (1, 0), (3, 0), (0, 0))
+
+
+def edge_kernel(
+    edge_hbm, w_hbm, rev_hbm, w_post_hbm, w_out_hbm, atom_hbm, count_hbm, owner_hbm, out_ref,
+    edge_ref, w_ref, rev_ref, w_post_ref, w_out_ref, atom_ref, count_ref, owner_ref, load, first, spread, midway, moved, landed, detour, total, rev_wide,
     send1, recv1, send2, recv2, send3, recv3, send4, recv4, recv5, send6,
+    message, match, place, pair_out, pair_in, mine,
+    left_y_out, left_y_in, left_x_out, left_x_in, left_keep,
+    right_x_out, right_x_in, right_y_out, right_y_in, right_keep,
+    pair_send, pair_recv, left_y_send, left_y_recv, left_x_send, left_x_recv,
+    right_x_send, right_x_recv, right_y_send, right_y_recv,
 ):
     y, xh, c, z, xl = where_am_i()
     zy, z0 = z // 2, lax.rem(z, 2)
@@ -41,8 +50,14 @@
     far = jnp.logical_not(alone)
     leaf = jnp.logical_not(relay)
     rows, width = edge_ref.shape
+    layers = w_ref.shape[0]
     chunk = rows // CHUNKS
     piece = chunk // 4
+
+    edges, message_width = message.shape
+    half = message_width // 2
+    other = (y, xh, 1 - c, z, xl)
+    across = (y, 1 - xh, c, z, xl)
 
     def along_y(step):
         return (lax.rem(y + step, 4), xh, c, z, xl)
@@ -62,10 +77,27 @@
     for step in range(1, 8):
         greet(along_z(step))
     greet(along_x(1))
+    greet(other)
 
     @pl.when(jnp.logical_not(settled))
     def _():
         greet(along_x(0))
+        greet(across)
+
+    head, tail = pl.ds(0, chunk), pl.ds(chunk, rows - chunk)
+    load_w = pltpu.make_async_copy(w_hbm, w_ref, load.at[0])
+    load_head = pltpu.make_async_copy(edge_hbm.at[head], edge_ref.at[head], load.at[1])
+    load_tail = pltpu.make_async_copy(edge_hbm.at[tail], edge_ref.at[tail], load.at[2])
+    load_rev = pltpu.make_async_copy(rev_hbm, rev_ref, load.at[3])
+    load_rest = [
+        pltpu.make_async_copy(out, into, load.at[4 + index])
+        for index, (out, into) in enumerate((
+            (w_post_hbm, w_post_ref), (w_out_hbm, w_out_ref), (atom_hbm, atom_ref),
+            (count_hbm, count_ref), (owner_hbm, owner_ref),
+        ))
+    ]
+    for item in (load_head, load_w, load_rev, load_tail, *load_rest):
+        item.start()
 
     def remote(src, dst, send, recv, device):
         return pltpu.make_async_remote_copy(
@@ -164,7 +196,7 @@
     def embed(g):
         here = pl.ds(pl.multiple_of(g * chunk, chunk), chunk)
         hidden = edge_ref[here, :]
-        for index in range(w_ref.shape[0]):
+        for index in range(layers):
             hidden = layer(hidden, w_ref[index])
         first[here, :] = hidden
 
@@ -211,6 +243,19 @@
             else:
                 when(far, lambda: got3(g, slot).wait_recv())
 
+    def sent(x_first, g):
+        for m in range(4):
+            when(far2(x_first, m), lambda: copy2(x_first, g, m).wait_send())
+        for hop in range(8):
+            if far3(x_first, hop) is not False:
+                when(far3(x_first, hop), lambda: copy3(x_first, g, hop).wait_send())
+
+        @pl.when(relay)
+        def _():
+            detour_out(x_first, g).wait_send()
+            detour_on(x_first, g).wait_send()
+
+
     def by_kind(work, g):
         @pl.when(lax.rem(g, 2) == 0)
         def _():
@@ -247,6 +292,16 @@
         @pl.when(i == 2)
         def _():
             total[...] = jnp.zeros_like(total)
+            for item in load_rest:
+                item.wait()
+            atoms = atom_ref[...]
+            owner = jnp.zeros_like(atoms)
+            for k in range(owner_ref.shape[1]):
+                owner = jnp.where(atoms // SUB == k, owner_ref[:, k : k + 1], owner)
+            edge = lax.broadcasted_iota(jnp.int32, atoms.shape, 1)
+            place[...] = jnp.where(edge < count_ref[...], owner, -1)
+            row = lax.broadcasted_iota(jnp.int32, (SUB, edges), 0)
+            match[...] = jnp.where(row == atoms % SUB, 1.0, 0.0).astype(BF16)
 
         g = i - sum(LAGS[:3])
 
@@ -267,18 +322,46 @@
             slot, offset = lane // piece, lane % piece
             origin = g * chunk + ((y + 4 - slot) % 4) * piece + offset
 
+            def picked(some):
+                wide = jnp.concatenate([rev_wide[some, :]] * (chunk // 128), axis=1)
+                choose = jnp.where(wide == origin, 1.0, 0.0).astype(BF16)
+                return total[some, :] + jnp.dot(choose, block, preferred_element_type=F32)
+
             def add(t, carry):
                 some = pl.ds(pl.multiple_of(t * 256, 256), 256)
-                picked = jnp.concatenate([rev_wide[some, :]] * (chunk // 128), axis=1)
-                choose = jnp.where(picked == origin, 1.0, 0.0).astype(BF16)
-                total[some, :] += jnp.dot(choose, block, preferred_element_type=F32)
+                total[some, :] = picked(some)
                 return carry
 
-            lax.fori_loop(0, rows // 256, add, 0)
+            def tell(t, carry):
+                some = pl.ds(pl.multiple_of(t * 256, 256), 256)
+                both = first[some, :].astype(F32) + picked(some)
+                hidden = (both * HALF_ROOT).astype(BF16)
+                for index in range(layers):
+                    hidden = layer(hidden, w_post_ref[index])
+                message[some, :] = jnp.dot(
+                    hidden, w_out_ref[...], preferred_element_type=F32
+                ).astype(BF16)
+                return carry
+
+            @pl.when(g < CHUNKS - 1)
+            def _():
+                lax.fori_loop(0, rows // 256, add, 0)
+
+            @pl.when(g == CHUNKS - 1)
+            def _():
+                lax.fori_loop(0, rows // 256, tell, 0)
+
+            for step in range(1, 4):
+                copy1(g, step).wait_send()
+                copy4(g, step).wait_send()
+            by_kind(sent, g)
 
         return carry
 
+    load_head.wait()
+    load_w.wait()
     embed(0)
+    load_rev.wait()
 
     def widen(t, carry):
         part = pl.ds(pl.multiple_of(t * 128, 128), 128)
@@ -286,109 +369,11 @@
         return carry
 
     lax.fori_loop(0, rows // 128, widen, 0)
-    pl.semaphore_wait(barrier, jnp.where(settled, 11, 12))
+    load_tail.wait()
+    pl.semaphore_wait(barrier, jnp.where(settled, 12, 14))
     lax.fori_loop(0, CHUNKS + sum(LAGS), stage, 0)
 
-    def sent(x_first, g):
-        for m in range(4):
-            when(far2(x_first, m), lambda: copy2(x_first, g, m).wait_send())
-        for hop in range(8):
-            if far3(x_first, hop) is not False:
-                when(far3(x_first, hop), lambda: copy3(x_first, g, hop).wait_send())
-
-        @pl.when(relay)
-        def _():
-            detour_out(x_first, g).wait_send()
-            detour_on(x_first, g).wait_send()
-
-
-    def finish(g, carry):
-        here = pl.ds(pl.multiple_of(g * chunk, chunk), chunk)
-        both = first[here, :].astype(F32) + total[here, :]
-        joined_ref[here, :] = (both * HALF_ROOT).astype(BF16)
-        for step in range(1, 4):
-            copy1(g, step).wait_send()
-            copy4(g, step).wait_send()
-        by_kind(sent, g)
-        return carry
-
-    lax.fori_loop(0, CHUNKS, finish, 0)
-
-
-def mirror(edge, w_pre, rev):
-    rows, width = edge.shape
-    piece = rows // CHUNKS // 4
-    pieces = lambda n: pltpu.VMEM((CHUNKS, n, piece, width), BF16)
-    sems = lambda n: pltpu.SemaphoreType.DMA((CHUNKS, n))
-    vmem = pl.BlockSpec(memory_space=pltpu.VMEM)
-    return pl.pallas_call(
-        mirror_kernel,
-        name="mirror",
-        out_shape=jax.ShapeDtypeStruct((rows, width), BF16),
-        in_specs=[vmem] * 3,
-        out_specs=vmem,
-        scratch_shapes=[
-            pltpu.VMEM((rows, width), BF16),
-            pieces(4), pieces(8), pieces(4), pieces(4),
-            pltpu.VMEM((CHUNKS, piece, width), BF16),
-            pltpu.VMEM((rows, width), F32),
-            pltpu.VMEM((rows, 128), jnp.int32),
-            sems(4), sems(4), sems(4), sems(8), sems(8), sems(4), sems(4), sems(4),
-            pltpu.SemaphoreType.DMA((CHUNKS,)), pltpu.SemaphoreType.DMA((CHUNKS,)),
-        ],
-        compiler_params=pltpu.CompilerParams(
-            collective_id=0, has_side_effects=True, vmem_limit_bytes=40 << 20
-        ),
-    )(edge, w_pre, rev)
-
-
-HOPS = ((2, 1), (1, 1), (3, 1), (0, 1), (2, 0), (1, 0), (3, 0), (0, 0))
-
-
-def owner_kernel(
-    joined_ref, w_ref, w_out_ref, atom_ref, count_ref, owner_ref, out_ref,
-    message, match, place, pair_out, pair_in, mine,
-    left_y_out, left_y_in, left_x_out, left_x_in, left_keep,
-    right_x_out, right_x_in, right_y_out, right_y_in, right_keep,
-    pair_send, pair_recv, left_y_send, left_y_recv, left_x_send, left_x_recv,
-    right_x_send, right_x_recv, right_y_send, right_y_recv,
-):
-    y, xh, c, z, xl = where_am_i()
-    edges, width = message.shape
-    half = width // 2
-    other = (y, xh, 1 - c, z, xl)
-    across = (y, 1 - xh, c, z, xl)
-
-    def along_y(step):
-        return (lax.rem(y + step, 4), xh, c, z, xl)
-
-    barrier = pltpu.get_barrier_semaphore()
-    for device in (other, across, along_y(1), along_y(2), along_y(3)):
-        pl.semaphore_signal(barrier, inc=1, device_id=device, device_id_type=MESH)
-
-    atoms = atom_ref[...]
-    owner = jnp.zeros_like(atoms)
-    for k in range(owner_ref.shape[1]):
-        owner = jnp.where(atoms // SUB == k, owner_ref[0, k], owner)
-    edge = lax.broadcasted_iota(jnp.int32, atoms.shape, 1)
-    place[...] = jnp.where(edge < count_ref[0, 0], owner, -1)
-    row = lax.broadcasted_iota(jnp.int32, (SUB, edges), 0)
-    match[...] = jnp.where(row == atoms % SUB, 1.0, 0.0).astype(BF16)
-
-    def tell(t, carry):
-        some = pl.ds(pl.multiple_of(t * 512, 512), 512)
-        hidden = joined_ref[some, :]
-        for index in range(w_ref.shape[0]):
-            hidden = layer(hidden, w_ref[index])
-        message[some, :] = jnp.dot(
-            hidden, w_out_ref[...], preferred_element_type=F32
-        ).astype(BF16)
-        return carry
-
-    lax.fori_loop(0, edges // 512, tell, 0)
-    pl.semaphore_wait(barrier, 5)
-
-    def copy(out, into, send, recv, index, device):
+    def owner_copy(out, into, send, recv, index, device):
         return pltpu.make_async_remote_copy(
             src_ref=out.at[index], dst_ref=into.at[index],
             send_sem=send.at[index], recv_sem=recv.at[index],
@@ -396,21 +381,21 @@
         )
 
     def pair_copy(hop):
-        return copy(pair_out, pair_in, pair_send, pair_recv, hop, other)
+        return owner_copy(pair_out, pair_in, pair_send, pair_recv, hop, other)
 
     def left_y(dy, dx):
-        return copy(
+        return owner_copy(
             left_y_out, left_y_in, left_y_send, left_y_recv, 2 * (dy - 1) + dx, along_y(dy)
         )
 
     def left_x():
-        return copy(left_x_out, left_x_in, left_x_send, left_x_recv, 0, across)
+        return owner_copy(left_x_out, left_x_in, left_x_send, left_x_recv, 0, across)
 
     def right_x(dy):
-        return copy(right_x_out, right_x_in, right_x_send, right_x_recv, dy, across)
+        return owner_copy(right_x_out, right_x_in, right_x_send, right_x_recv, dy, across)
 
     def right_y(dy):
-        return copy(right_y_out, right_y_in, right_y_send, right_y_recv, dy - 1, along_y(dy))
+        return owner_copy(right_y_out, right_y_in, right_y_send, right_y_recv, dy - 1, along_y(dy))
 
     def compute(hop):
         dy, dx = HOPS[hop]
@@ -481,39 +466,51 @@
             left_y(dy, dx).wait_send()
 
 
-def owner_sums(joined, w_post, w_out, atoms, count, owners):
-    edges, width = joined.shape[0], w_out.shape[1]
-    whole = lambda n, kind=BF16: pltpu.VMEM((n, SUB, width), kind)
-    halves = lambda n, kind=BF16: pltpu.VMEM((n, SUB, width // 2), kind)
+def edge_block(*operands):
+    edge, w_pre, rev, w_post, w_out, atoms, count, owners = operands
+    rows, width = edge.shape
+    message_width = w_out.shape[1]
+    piece = rows // CHUNKS // 4
+    pieces = lambda n: pltpu.VMEM((CHUNKS, n, piece, width), BF16)
+    grid_sems = lambda n: pltpu.SemaphoreType.DMA((CHUNKS, n))
+    whole = lambda n, kind=BF16: pltpu.VMEM((n, SUB, message_width), kind)
+    halves = lambda n, kind=BF16: pltpu.VMEM((n, SUB, message_width // 2), kind)
     sems = lambda n: pltpu.SemaphoreType.DMA((n,))
-    vmem = pl.BlockSpec(memory_space=pltpu.VMEM)
-    smem = pl.BlockSpec(memory_space=pltpu.SMEM)
     return pl.pallas_call(
-        owner_kernel,
-        name="owner_sums",
-        out_shape=jax.ShapeDtypeStruct((SUB, width), BF16),
-        in_specs=[vmem, vmem, vmem, vmem, smem, smem],
-        out_specs=vmem,
+        edge_kernel,
+        name="edge_block",
+        out_shape=jax.ShapeDtypeStruct((SUB, message_width), BF16),
+        in_specs=[pl.BlockSpec(memory_space=pltpu.HBM)] * len(operands),
+        out_specs=pl.BlockSpec(memory_space=pltpu.VMEM),
         scratch_shapes=[
-            pltpu.VMEM((edges, width), BF16),
-            pltpu.VMEM((SUB, edges), BF16),
+            *(pltpu.VMEM(operand.shape, operand.dtype) for operand in operands),
+            sems(9),
+            pltpu.VMEM((rows, width), BF16),
+            pieces(4), pieces(8), pieces(4), pieces(4),
+            pltpu.VMEM((CHUNKS, piece, width), BF16),
+            pltpu.VMEM((rows, width), F32),
+            pltpu.VMEM((rows, 128), jnp.int32),
+            *(grid_sems(n) for n in (4, 4, 4, 8, 8, 4, 4, 4)),
+            sems(CHUNKS), sems(CHUNKS),
+            pltpu.VMEM((rows, message_width), BF16),
+            pltpu.VMEM((SUB, rows), BF16),
             pltpu.VMEM(atoms.shape, jnp.int32),
             whole(8), whole(8), whole(2, F32),
             halves(6), halves(6), halves(1), halves(1), halves(2, F32),
             halves(4), halves(4), halves(3), halves(3), halves(4, F32),
-            sems(8), sems(8), sems(6), sems(6), sems(1), sems(1),
-            sems(4), sems(4), sems(3), sems(3),
+            *(sems(n) for n in (8, 8, 6, 6, 1, 1, 4, 4, 3, 3)),
         ],
         compiler_params=pltpu.CompilerParams(
-            collective_id=1, has_side_effects=True, vmem_limit_bytes=32 << 20
+            collective_id=0, has_side_effects=True, vmem_limit_bytes=VMEM_BYTES
         ),
-    )(joined, w_post, w_out, atoms, count, owners)
+    )(*operands)
 
 
 def shards(edge_feat, tile_counts, reverse_rows, incidence, owner_map, w_pre, w_post, w_out):
-    joined = mirror(edge_feat[0, 0], w_pre, reverse_rows[0])
-    sums = owner_sums(joined, w_post, w_out, incidence[0], tile_counts, owner_map)
-    return sums[None]
+    return edge_block(
+        edge_feat[0, 0], w_pre, reverse_rows[0], w_post, w_out,
+        incidence[0], tile_counts, owner_map,
+    )[None]
 
 
 def solution(mesh):

time: 108 us -> 110 us (1.019)
  Pallas kernels: 102 us -> 107 us
  local copies, waits for them, and re-layouts: 4.36 us -> 1.57 us
    pallas_call x2 -> x1, Pallas kernels: 102 us -> 107 us  [edge_block(): pl.pallas_call(edge_kernel, name='edge_block', out_shape=jax.ShapeDtypeSt...]
    unnamed x15 -> x1, local copies, waits for them, and re-layouts: 4.36 us -> 1.57 us
where the time goes in v5:
time: 110 us
  Pallas kernels  107 us (97%)
  local copies, waits for them, and re-layouts  1.57 us (1%)
    pallas_call x1, Pallas kernels, edge_block(): pl.pallas_call(edge_kernel, name='edge_block', out_shape=jax.ShapeDtypeSt...  107 us

profile of v5, /device:TPU:1, one launch (start us, length us, event | category | flops | bytes accessed | tf_op | source)
XLA Modules:
  0.0 109.7 jit_solution(7057306570780553133)
XLA Ops:
  0.7 107.5 %edge_block.1 = bf16[256,256]{1,0:T(8,128)(2,1)} custom-call(bf16[2048,512]{1,0:T(8,128)(2,1)} %bitcast.4, bf16[3,512,512]{2,1,0:T(8,128)(2,1)} %w_hbm.1, s32[1,2048]{1,0:T(1,128)} %bitcast.6, bf16[3,512,512]{2,1,0:T(8,128)(2,1)} %w_post_hbm.1, bf16[512,256]{1,0:T(8,128)(2,1)} %w_out_hbm.1, s32[1,2048]{1,0:T(1,128)} %bitcast.7, s32[1,1]{1,0:T(1,128)S(6)} %copy.10.count_hbm, ...), custom_call_target="tpu_custom_call" | custom-call | tf_op jit(solution)/shard_map/edge_block/pallas_call | solution.py:479
  108.2 1.6 %copy.11 = bf16[1,256,256]{2,1,0:T(8,128)(2,1)} copy(bf16[1,256,256]{2,1,0:T(8,128)(2,1)} %bitcast.5) | data formatting | bytes 262144

commit v6 on v5

--- a/solution.py
+++ b/solution.py
@@ -96,7 +96,7 @@
             (count_hbm, count_ref), (owner_hbm, owner_ref),
         ))
     ]
-    for item in (load_head, load_w, load_rev, load_tail, *load_rest):
+    for item in (load_head, load_w, load_rev):
         item.start()
 
     def remote(src, dst, send, recv, device):
@@ -291,7 +291,12 @@
 
         @pl.when(i == 2)
         def _():
+            for item in load_rest:
+                item.start()
             total[...] = jnp.zeros_like(total)
+
+        @pl.when(i == CHUNKS + 3)
+        def _():
             for item in load_rest:
                 item.wait()
             atoms = atom_ref[...]
@@ -328,13 +333,13 @@
                 return total[some, :] + jnp.dot(choose, block, preferred_element_type=F32)
 
             def add(t, carry):
-                some = pl.ds(pl.multiple_of(t * 256, 256), 256)
+                some = pl.ds(pl.multiple_of(t * 1024, 1024), 1024)
                 total[some, :] = picked(some)
                 return carry
 
             def tell(t, carry):
-                some = pl.ds(pl.multiple_of(t * 256, 256), 256)
-                both = first[some, :].astype(F32) + picked(some)
+                some = pl.ds(pl.multiple_of(t * 1024, 1024), 1024)
+                both = first[some, :].astype(F32) + total[some, :]
                 hidden = (both * HALF_ROOT).astype(BF16)
                 for index in range(layers):
                     hidden = layer(hidden, w_post_ref[index])
@@ -343,23 +348,17 @@
                 ).astype(BF16)
                 return carry
 
-            @pl.when(g < CHUNKS - 1)
-            def _():
-                lax.fori_loop(0, rows // 256, add, 0)
+            lax.fori_loop(0, rows // 1024, add, 0)
 
             @pl.when(g == CHUNKS - 1)
             def _():
-                lax.fori_loop(0, rows // 256, tell, 0)
-
-            for step in range(1, 4):
-                copy1(g, step).wait_send()
-                copy4(g, step).wait_send()
-            by_kind(sent, g)
+                lax.fori_loop(0, rows // 1024, tell, 0)
 
         return carry
 
     load_head.wait()
     load_w.wait()
+    load_tail.start()
     embed(0)
     load_rev.wait()
 
@@ -425,13 +424,7 @@
         else:
             right_keep[dy] = chip_sum[:, half:]
 
-    compute(0)
-    for hop in range(1, 8):
-        compute(hop)
-        pass_on(hop - 1)
-    pass_on(7)
-
-    for dy in (2, 1, 3):
+    def turn_right(dy):
         right_x(dy).wait_recv()
         right_y_out[dy - 1] = (right_keep[dy] + right_x_in[dy].astype(F32)).astype(BF16)
         right_y(dy).start()
@@ -443,8 +436,16 @@
             value = value + left_y_in[2 * (dy - 1) + dx].astype(F32)
         return value
 
+    compute(0)
+    for hop in range(1, 8):
+        compute(hop)
+        pass_on(hop - 1)
+        if hop >= 6:
+            turn_right(HOPS[hop - 2][0])
     left_x_out[0] = gathered(1).astype(BF16)
     left_x().start()
+    pass_on(7)
+    turn_right(HOPS[6][0])
     left_sum = gathered(0)
     right_x(0).wait_recv()
     right_sum = right_keep[0] + right_x_in[0].astype(F32)
@@ -455,6 +456,14 @@
     left_x().wait_recv()
     out_ref[:, :half] = (left_sum + left_x_in[0].astype(F32)).astype(BF16)
 
+    def settle(g, carry):
+        for step in range(1, 4):
+            copy1(g, step).wait_send()
+            copy4(g, step).wait_send()
+        by_kind(sent, g)
+        return carry
+
+    lax.fori_loop(0, CHUNKS, settle, 0)
     for hop in range(8):
         pair_copy(hop).wait_send()
     left_x().wait_send()

time: 110 us -> 103 us (0.936)
  Pallas kernels: 107 us -> 101 us
    pallas_call x1, Pallas kernels: 107 us -> 101 us  [edge_block(): pl.pallas_call(edge_kernel, name='edge_block', out_shape=jax.ShapeDtypeSt...]
where the time goes in v6:
time: 103 us
  Pallas kernels  101 us (98%)
  local copies, waits for them, and re-layouts  1.57 us (2%)
    pallas_call x1, Pallas kernels, edge_block(): pl.pallas_call(edge_kernel, name='edge_block', out_shape=jax.ShapeDtypeSt...  101 us

profile of v6, /device:TPU:1, one launch (start us, length us, event | category | flops | bytes accessed | tf_op | source)
XLA Modules:
  0.0 103.1 jit_solution(8209569047849738900)
XLA Ops:
  0.7 100.8 %edge_block.1 = bf16[256,256]{1,0:T(8,128)(2,1)} custom-call(bf16[2048,512]{1,0:T(8,128)(2,1)} %bitcast.4, bf16[3,512,512]{2,1,0:T(8,128)(2,1)} %w_hbm.1, s32[1,2048]{1,0:T(1,128)} %bitcast.6, bf16[3,512,512]{2,1,0:T(8,128)(2,1)} %w_post_hbm.1, bf16[512,256]{1,0:T(8,128)(2,1)} %w_out_hbm.1, s32[1,2048]{1,0:T(1,128)} %bitcast.7, s32[1,1]{1,0:T(1,128)S(6)} %copy.10.count_hbm, ...), custom_call_target="tpu_custom_call" | custom-call | tf_op jit(solution)/shard_map/edge_block/pallas_call | solution.py:488
  101.5 1.6 %copy.11 = bf16[1,256,256]{2,1,0:T(8,128)(2,1)} copy(bf16[1,256,256]{2,1,0:T(8,128)(2,1)} %bitcast.5) | data formatting | bytes 262144

commit v7 on v6

--- a/solution.py
+++ b/solution.py
@@ -333,7 +333,7 @@
                 return total[some, :] + jnp.dot(choose, block, preferred_element_type=F32)
 
             def add(t, carry):
-                some = pl.ds(pl.multiple_of(t * 1024, 1024), 1024)
+                some = pl.ds(pl.multiple_of(t * 2048, 2048), 2048)
                 total[some, :] = picked(some)
                 return carry
 
@@ -348,7 +348,7 @@
                 ).astype(BF16)
                 return carry
 
-            lax.fori_loop(0, rows // 1024, add, 0)
+            lax.fori_loop(0, rows // 2048, add, 0)
 
             @pl.when(g == CHUNKS - 1)
             def _():

time: 103 us -> 103 us (level)
  no operation moved by 1% of the time
where the time goes in v7:
time: 103 us
  Pallas kernels  101 us (98%)
  local copies, waits for them, and re-layouts  1.57 us (2%)
    pallas_call x1, Pallas kernels, edge_block(): pl.pallas_call(edge_kernel, name='edge_block', out_shape=jax.ShapeDtypeSt...  101 us

profile of v7, /device:TPU:1, one launch (start us, length us, event | category | flops | bytes accessed | tf_op | source)
XLA Modules:
  0.0 102.9 jit_solution(10990349619909267312)
XLA Ops:
  0.7 100.7 %edge_block.1 = bf16[256,256]{1,0:T(8,128)(2,1)} custom-call(bf16[2048,512]{1,0:T(8,128)(2,1)} %bitcast.4, bf16[3,512,512]{2,1,0:T(8,128)(2,1)} %w_hbm.1, s32[1,2048]{1,0:T(1,128)} %bitcast.6, bf16[3,512,512]{2,1,0:T(8,128)(2,1)} %w_post_hbm.1, bf16[512,256]{1,0:T(8,128)(2,1)} %w_out_hbm.1, s32[1,2048]{1,0:T(1,128)} %bitcast.7, s32[1,1]{1,0:T(1,128)S(6)} %copy.10.count_hbm, ...), custom_call_target="tpu_custom_call" | custom-call | tf_op jit(solution)/shard_map/edge_block/pallas_call | solution.py:488
  101.4 1.6 %copy.11 = bf16[1,256,256]{2,1,0:T(8,128)(2,1)} copy(bf16[1,256,256]{2,1,0:T(8,128)(2,1)} %bitcast.5) | data formatting | bytes 262144
